TPU v7x, 128 devices: a whole 4x4x4 slice. The times are simulated.
128 devices in a mesh: aux: 8 (over x, core), orb: 16 (over y, z).
Axes of the slice: x: 4, y: 4, z: 4, core: 2. Of those that a mesh axis runs over, the one named last changes fastest.
Arguments:
- raw_ints: bfloat16 [8, 16, 1024, 1536], P(None, 'orb', 'aux'), may hold values from -0.625 to 0.625
- fit_inverse: bfloat16 [128, 1024, 1024], P(('aux', 'orb')), may hold values from -0.1875 to 0.1875
- pair_orbs: int32 [2048, 2], P(('aux', 'orb')), may hold values from 0 to 15, all different within a row; in each aligned block of 16 rows (0 to 15, 16 to 31, ...) at most 4 rows name the same one
- pno_coef: bfloat16 [2048, 2, 32, 1536], P(('aux', 'orb')), may hold values from -0.15625 to 0.15625
- pno_energy: float32 [2048, 2, 32], P(('aux', 'orb')), may hold values from 0.3 to 6
- occ_energy: float32 [128], replicated, may hold values from -1.5 to -0.3
- fit_offset: int32 [128], replicated, may hold values from 0 to 255
Outputs:
- amplitude: float32 [2048, 1024], P(('aux', 'orb'))
- energy: float32 [2048], P(('aux', 'orb'))
Inputs may be any that keep to these rules, and one draw needn't show every extreme that they name: `pair_orbs`: each entry is an orbital's index within the pair's region; the two entries of a row differ; among the rows of one device no orbital is named more than 4 times.
All inputs are finite; a program needn't handle non-finite values.
Results may differ from a plain program's by a relative error of at most 0.0057.
Values may be sent and summed in bfloat16 or wider, within the bound.
A program may use at most 64 MiB of HBM per device.

v0:
```python
import jax
import jax.numpy as jnp
from jax import lax
from jax.sharding import PartitionSpec as P


def align_rows(shifted_in, begin_at):
    return lax.dynamic_slice_in_dim(shifted_in, begin_at, shifted_in.shape[1] * 2 // 3, 1)


def on_device(raw_ints, fit_inverse, pair_orbs, pno_coef, pno_energy, occ_energy, fit_offset):
    orb_count = lax.axis_size("orb")
    region = lax.axis_index("aux")
    inverse = fit_inverse[0]
    gathered = lax.all_to_all(raw_ints, "aux", split_axis=0, concat_axis=2, tiled=True)
    fitted = jnp.dot(inverse, gathered[0, 0], preferred_element_type=jnp.float32).astype(
        jnp.bfloat16
    )
    fit_rows = fitted.shape[0]
    pair_count = pair_orbs.shape[0]
    pno_count = pno_coef.shape[2]
    dom_count = pno_coef.shape[3]
    side_count = 2 * pair_count
    capacity = max(2, 4 * pair_count // orb_count)
    slot_count = orb_count * capacity
    side_orbs = pair_orbs.reshape(side_count)
    matches = side_orbs[:, None] == side_orbs[None, :]
    sequence = jnp.arange(side_count, dtype=jnp.int32)
    earlier = sequence[None, :] < sequence[:, None]
    position = jnp.sum(jnp.where(matches & earlier, 1, 0), axis=1)
    slot_index = side_orbs * capacity + position
    placing = jnp.where(
        slot_index[None, :] == jnp.arange(slot_count, dtype=jnp.int32)[:, None], 1.0, 0.0
    ).astype(jnp.bfloat16)
    outgoing = jnp.dot(
        placing,
        pno_coef.reshape(side_count, pno_count * dom_count),
        preferred_element_type=jnp.float32,
    ).astype(jnp.bfloat16)
    outgoing = outgoing.reshape(orb_count, capacity, pno_count, dom_count)
    projected = jnp.einsum(
        "scpd,fd->scpf",
        lax.all_to_all(outgoing, "orb", split_axis=0, concat_axis=0, tiled=True),
        fitted,
        preferred_element_type=jnp.float32,
    ).astype(jnp.bfloat16)
    returned = lax.all_to_all(projected, "orb", split_axis=0, concat_axis=0, tiled=True)
    side_blocks = jnp.dot(
        placing.T,
        returned.reshape(slot_count, pno_count * fit_rows),
        preferred_element_type=jnp.float32,
    ).astype(jnp.bfloat16)
    side_blocks = side_blocks.reshape(pair_count, 2, pno_count, fit_rows)
    orb_total = occ_energy.shape[0]
    global_orb = region * orb_count + pair_orbs
    selector = global_orb[:, :, None] == jnp.arange(orb_total, dtype=jnp.int32)[None, None, :]
    offsets = jnp.sum(jnp.where(selector, fit_offset[None, None, :], 0), axis=2)
    occupied = jnp.sum(jnp.where(selector, occ_energy[None, None, :], 0.0), axis=2)
    margin = fit_rows // 4
    shift_rows = offsets[:, 0] - offsets[:, 1]
    padded = jnp.pad(side_blocks[:, 1], ((0, 0), (0, 0), (margin, margin)))
    aligned = jax.vmap(align_rows)(padded, margin + shift_rows)
    coupling = jnp.einsum(
        "npr,nqr->npq", side_blocks[:, 0], aligned, preferred_element_type=jnp.float32
    )
    denominator = (
        pno_energy[:, 0, :, None]
        + pno_energy[:, 1, None, :]
        - occupied[:, 0, None, None]
        - occupied[:, 1, None, None]
    )
    amplitude = -coupling / denominator
    energy = jnp.sum(coupling * (2.0 * amplitude - jnp.swapaxes(amplitude, 1, 2)), axis=(1, 2))
    return (amplitude.reshape(pair_count, pno_count * pno_count), energy)


def solution(mesh):
    return jax.shard_map(
        on_device,
        mesh=mesh,
        in_specs=(
            P(None, "orb", "aux", None),
            P(("aux", "orb"), None, None),
            P(("aux", "orb"), None),
            P(("aux", "orb"), None, None, None),
            P(("aux", "orb"), None, None),
            P(),
            P(),
        ),
        out_specs=(P(("aux", "orb"), None), P(("aux", "orb"))),
        check_vma=False,
    )
```

profile of v0, /device:TPU:1, one launch (start us, length us, event | category | flops | bytes accessed | tf_op | source)
XLA Modules:
  0.0 265.0 jit_solution(12260790169756943740)
XLA Ops:
  0.7 5.9 %all-to-all-start.1 = ((bf16[8,1,128,1536]{3,2,1,0:T(8,128)(2,1)}), bf16[8,1,128,1536]{3,2,1,0:T(8,128)(2,1)}, u32[]{:S(2)}, u32[]{:S(2)}) async-start(bf16[8,1,128,1536]{3,2,1,0:T(8,128)(2,1)} %param.7), calls=%async_computation.1 | async-start | bytes 6291456 | tf_op jit(solution)/shard_map/all_to_all | solution.py:15
  6.8 3.6 %copy.26 = bf16[4,8,32,1536]{3,1,2,0:T(8,128)(2,1)S(1)} copy(bf16[4,8,32,1536]{3,2,1,0:T(8,128)(2,1)} %bitcast.59) | data formatting | bytes 6291456
  12.4 4.9 %copy.27 = bf16[8,8,32,1536]{3,2,1,0:T(8,128)(2,1)} copy(bf16[8,8,32,1536]{3,1,2,0:T(8,128)(2,1)S(1)} %bitcast.53) | data formatting | bytes 12582912
  17.3 27.0 %all-to-all-done.1 = bf16[8,1,128,1536]{3,2,1,0:T(8,128)(2,1)} async-done(((bf16[8,1,128,1536]{3,2,1,0:T(8,128)(2,1)}), bf16[8,1,128,1536]{3,2,1,0:T(8,128)(2,1)}, u32[]{:S(2)}, u32[]{:S(2)}) %all-to-all-start.1) | async-done | bytes 3145760 | tf_op jit(solution)/shard_map/all_to_all | solution.py:15
  44.3 79.9 %all_to_all.19 = bf16[16,4,32,1536]{3,2,1,0:T(8,128)(2,1)} all-to-all(bf16[16,4,32,1536]{3,2,1,0:T(8,128)(2,1)} %bitcast.52), channel_id=1, replica_groups=mesh['aux'=8,'orb'=16] {'orb'}, dimensions={0} | all-to-all | bytes 12582912 | tf_op jit(solution)/shard_map/all_to_all | solution.py:43
  124.2 15.3 %convolution_convert_fusion.3 = bf16[16,4,32,1024]{3,2,1,0:T(8,128)(2,1)} fusion(bf16[16,4,32,1536]{3,2,1,0:T(8,128)(2,1)} %all_to_all.19, bf16[1024,1536]{1,0:T(8,128)(2,1)} %bitcast.1, bf16[1,1024,1024]{2,1,0:T(8,128)(2,1)S(1)} %copy-done), kind=kOutput, calls=%fused_computation.6 | convolution fusion | flops 9667346432 | bytes 15728640 | tf_op jit(solution)/shard_map/scpd,fd->scpf/dot_general | solution.py:41
  139.5 4.9 %all-to-all-start.2 = ((bf16[16,4,32,1024]{3,2,1,0:T(8,128)(2,1)}), bf16[16,4,32,1024]{3,2,1,0:T(8,128)(2,1)}, u32[]{:S(2)}, u32[]{:S(2)}) async-start(bf16[16,4,32,1024]{3,2,1,0:T(8,128)(2,1)} %convolution_convert_fusion.3), calls=%async_computation.2 | async-start | bytes 8388608 | tf_op jit(solution)/shard_map/all_to_all | solution.py:47
  144.8 50.8 %all-to-all-done.2 = bf16[16,4,32,1024]{3,2,1,0:T(8,128)(2,1)} async-done(((bf16[16,4,32,1024]{3,2,1,0:T(8,128)(2,1)}), bf16[16,4,32,1024]{3,2,1,0:T(8,128)(2,1)}, u32[]{:S(2)}, u32[]{:S(2)}) %all-to-all-start.2) | async-done | bytes 4194336 | tf_op jit(solution)/shard_map/all_to_all | solution.py:47
  195.6 4.6 %copy.28 = bf16[8,8,32,1024]{3,1,2,0:T(8,128)(2,1)S(1)} copy(bf16[8,8,32,1024]{3,2,1,0:T(8,128)(2,1)} %bitcast.25) | data formatting | bytes 8388608
  204.9 56.3 %while.1 = (s32[]{:T(128)}, bf16[16,32,1536]{2,1,0:T(8,128)(2,1)}, s32[16,3]{0,1:T(4,128)S(1)}, bf16[16,32,1024]{2,1,0:T(8,128)(2,1)}, s32[]{:T(128)}) while((s32[]{:T(128)}, bf16[16,32,1536]{2,1,0:T(8,128)(2,1)}, s32[16,3]{0,1:T(4,128)S(1)}, bf16[16,32,1024]{2,1,0:T(8,128)(2,1)}, s32[]{:T(128)}) %tuple.26), condition=%wide.while_cond, body=%wide.while_body.sunk | while | flops 2 | bytes 132713 | solution.py:8
  209.0 2.9 %dynamic-slice_dynamic-update-slice_fusion.2 = bf16[16,32,1024]{2,1,0:T(8,128)(2,1)} fusion(bf16[16,32,1024]{2,1,0:T(8,128)(2,1)} %get-tuple-element.63, s32[]{:T(128)} %get-tuple-element.60, bf16[16,32,1536]{2,1,0:T(8,128)(2,1)} %get-tuple-element.66, s32[]{:T(128)} %bitcast.50, s32[]{:T(128)} %bitcast.51), kind=kLoop, calls=%fused_computation.clone.1 | loop fusion | bytes 132608 | tf_op jit(solution)/shard_map/vmap()/gather
  212.5 2.9 %dynamic-slice_dynamic-update-slice_fusion.2 = bf16[16,32,1024]{2,1,0:T(8,128)(2,1)} fusion(bf16[16,32,1024]{2,1,0:T(8,128)(2,1)} %get-tuple-element.63, s32[]{:T(128)} %get-tuple-element.60, bf16[16,32,1536]{2,1,0:T(8,128)(2,1)} %get-tuple-element.66, s32[]{:T(128)} %bitcast.50, s32[]{:T(128)} %bitcast.51), kind=kLoop, calls=%fused_computation.clone.1 | loop fusion | bytes 132608 | tf_op jit(solution)/shard_map/vmap()/gather
  219.6 2.9 %dynamic-slice_dynamic-update-slice_fusion.2 = bf16[16,32,1024]{2,1,0:T(8,128)(2,1)} fusion(bf16[16,32,1024]{2,1,0:T(8,128)(2,1)} %get-tuple-element.63, s32[]{:T(128)} %get-tuple-element.60, bf16[16,32,1536]{2,1,0:T(8,128)(2,1)} %get-tuple-element.66, s32[]{:T(128)} %bitcast.50, s32[]{:T(128)} %bitcast.51), kind=kLoop, calls=%fused_computation.clone.1 | loop fusion | bytes 132608 | tf_op jit(solution)/shard_map/vmap()/gather
  223.1 2.9 %dynamic-slice_dynamic-update-slice_fusion.2 = bf16[16,32,1024]{2,1,0:T(8,128)(2,1)} fusion(bf16[16,32,1024]{2,1,0:T(8,128)(2,1)} %get-tuple-element.63, s32[]{:T(128)} %get-tuple-element.60, bf16[16,32,1536]{2,1,0:T(8,128)(2,1)} %get-tuple-element.66, s32[]{:T(128)} %bitcast.50, s32[]{:T(128)} %bitcast.51), kind=kLoop, calls=%fused_computation.clone.1 | loop fusion | bytes 132608 | tf_op jit(solution)/shard_map/vmap()/gather
  226.6 2.9 %dynamic-slice_dynamic-update-slice_fusion.2 = bf16[16,32,1024]{2,1,0:T(8,128)(2,1)} fusion(bf16[16,32,1024]{2,1,0:T(8,128)(2,1)} %get-tuple-element.63, s32[]{:T(128)} %get-tuple-element.60, bf16[16,32,1536]{2,1,0:T(8,128)(2,1)} %get-tuple-element.66, s32[]{:T(128)} %bitcast.50, s32[]{:T(128)} %bitcast.51), kind=kLoop, calls=%fused_computation.clone.1 | loop fusion | bytes 132608 | tf_op jit(solution)/shard_map/vmap()/gather
  230.1 2.9 %dynamic-slice_dynamic-update-slice_fusion.2 = bf16[16,32,1024]{2,1,0:T(8,128)(2,1)} fusion(bf16[16,32,1024]{2,1,0:T(8,128)(2,1)} %get-tuple-element.63, s32[]{:T(128)} %get-tuple-element.60, bf16[16,32,1536]{2,1,0:T(8,128)(2,1)} %get-tuple-element.66, s32[]{:T(128)} %bitcast.50, s32[]{:T(128)} %bitcast.51), kind=kLoop, calls=%fused_computation.clone.1 | loop fusion | bytes 132608 | tf_op jit(solution)/shard_map/vmap()/gather
  233.7 2.9 %dynamic-slice_dynamic-update-slice_fusion.2 = bf16[16,32,1024]{2,1,0:T(8,128)(2,1)} fusion(bf16[16,32,1024]{2,1,0:T(8,128)(2,1)} %get-tuple-element.63, s32[]{:T(128)} %get-tuple-element.60, bf16[16,32,1536]{2,1,0:T(8,128)(2,1)} %get-tuple-element.66, s32[]{:T(128)} %bitcast.50, s32[]{:T(128)} %bitcast.51), kind=kLoop, calls=%fused_computation.clone.1 | loop fusion | bytes 132608 | tf_op jit(solution)/shard_map/vmap()/gather
  237.2 2.9 %dynamic-slice_dynamic-update-slice_fusion.2 = bf16[16,32,1024]{2,1,0:T(8,128)(2,1)} fusion(bf16[16,32,1024]{2,1,0:T(8,128)(2,1)} %get-tuple-element.63, s32[]{:T(128)} %get-tuple-element.60, bf16[16,32,1536]{2,1,0:T(8,128)(2,1)} %get-tuple-element.66, s32[]{:T(128)} %bitcast.50, s32[]{:T(128)} %bitcast.51), kind=kLoop, calls=%fused_computation.clone.1 | loop fusion | bytes 132608 | tf_op jit(solution)/shard_map/vmap()/gather
  240.7 2.9 %dynamic-slice_dynamic-update-slice_fusion.2 = bf16[16,32,1024]{2,1,0:T(8,128)(2,1)} fusion(bf16[16,32,1024]{2,1,0:T(8,128)(2,1)} %get-tuple-element.63, s32[]{:T(128)} %get-tuple-element.60, bf16[16,32,1536]{2,1,0:T(8,128)(2,1)} %get-tuple-element.66, s32[]{:T(128)} %bitcast.50, s32[]{:T(128)} %bitcast.51), kind=kLoop, calls=%fused_computation.clone.1 | loop fusion | bytes 132608 | tf_op jit(solution)/shard_map/vmap()/gather
  244.2 2.9 %dynamic-slice_dynamic-update-slice_fusion.2 = bf16[16,32,1024]{2,1,0:T(8,128)(2,1)} fusion(bf16[16,32,1024]{2,1,0:T(8,128)(2,1)} %get-tuple-element.63, s32[]{:T(128)} %get-tuple-element.60, bf16[16,32,1536]{2,1,0:T(8,128)(2,1)} %get-tuple-element.66, s32[]{:T(128)} %bitcast.50, s32[]{:T(128)} %bitcast.51), kind=kLoop, calls=%fused_computation.clone.1 | loop fusion | bytes 132608 | tf_op jit(solution)/shard_map/vmap()/gather
  247.7 2.9 %dynamic-slice_dynamic-update-slice_fusion.2 = bf16[16,32,1024]{2,1,0:T(8,128)(2,1)} fusion(bf16[16,32,1024]{2,1,0:T(8,128)(2,1)} %get-tuple-element.63, s32[]{:T(128)} %get-tuple-element.60, bf16[16,32,1536]{2,1,0:T(8,128)(2,1)} %get-tuple-element.66, s32[]{:T(128)} %bitcast.50, s32[]{:T(128)} %bitcast.51), kind=kLoop, calls=%fused_computation.clone.1 | loop fusion | bytes 132608 | tf_op jit(solution)/shard_map/vmap()/gather
  251.3 2.9 %dynamic-slice_dynamic-update-slice_fusion.2 = bf16[16,32,1024]{2,1,0:T(8,128)(2,1)} fusion(bf16[16,32,1024]{2,1,0:T(8,128)(2,1)} %get-tuple-element.63, s32[]{:T(128)} %get-tuple-element.60, bf16[16,32,1536]{2,1,0:T(8,128)(2,1)} %get-tuple-element.66, s32[]{:T(128)} %bitcast.50, s32[]{:T(128)} %bitcast.51), kind=kLoop, calls=%fused_computation.clone.1 | loop fusion | bytes 132608 | tf_op jit(solution)/shard_map/vmap()/gather
  254.8 2.9 %dynamic-slice_dynamic-update-slice_fusion.2 = bf16[16,32,1024]{2,1,0:T(8,128)(2,1)} fusion(bf16[16,32,1024]{2,1,0:T(8,128)(2,1)} %get-tuple-element.63, s32[]{:T(128)} %get-tuple-element.60, bf16[16,32,1536]{2,1,0:T(8,128)(2,1)} %get-tuple-element.66, s32[]{:T(128)} %bitcast.50, s32[]{:T(128)} %bitcast.51), kind=kLoop, calls=%fused_computation.clone.1 | loop fusion | bytes 132608 | tf_op jit(solution)/shard_map/vmap()/gather
  258.3 2.9 %dynamic-slice_dynamic-update-slice_fusion.2 = bf16[16,32,1024]{2,1,0:T(8,128)(2,1)} fusion(bf16[16,32,1024]{2,1,0:T(8,128)(2,1)} %get-tuple-element.63, s32[]{:T(128)} %get-tuple-element.60, bf16[16,32,1536]{2,1,0:T(8,128)(2,1)} %get-tuple-element.66, s32[]{:T(128)} %bitcast.50, s32[]{:T(128)} %bitcast.51), kind=kLoop, calls=%fused_computation.clone.1 | loop fusion | bytes 132608 | tf_op jit(solution)/shard_map/vmap()/gather
  (69 shorter events, 27.1 us)
Async XLA Ops:
  0.6 123.5 %copy-start = (bf16[1,1024,1024]{2,1,0:T(8,128)(2,1)S(1)}, bf16[1,1024,1024]{2,1,0:T(8,128)(2,1)}, u32[]{:S(2)}) copy-start(bf16[1,1024,1024]{2,1,0:T(8,128)(2,1)} %param.8) | copy-start | bytes 6291460
  0.6 6.0 %copy-start.3 = (s32[16,2]{0,1:T(2,128)S(1)}, s32[16,2]{0,1:T(2,128)}, u32[]{:S(2)}) copy-start(s32[16,2]{0,1:T(2,128)} %param.9) | copy-start | bytes 388
  0.7 43.6 %all-to-all-start.1 = ((bf16[8,1,128,1536]{3,2,1,0:T(8,128)(2,1)}), bf16[8,1,128,1536]{3,2,1,0:T(8,128)(2,1)}, u32[]{:S(2)}, u32[]{:S(2)}) async-start(bf16[8,1,128,1536]{3,2,1,0:T(8,128)(2,1)} %param.7), calls=%async_computation.1 | async-start | bytes 6291456 | tf_op jit(solution)/shard_map/all_to_all | solution.py:15
  139.5 4.9 %copy-start.4 = (s32[128]{0:T(128)S(1)}, s32[128]{0:T(128)}, u32[]{:S(2)}) copy-start(s32[128]{0:T(128)} %param.13) | copy-start | bytes 1540
  139.5 5.1 %copy-start.5 = (f32[128]{0:T(128)S(1)}, f32[128]{0:T(128)}, u32[]{:S(2)}) copy-start(f32[128]{0:T(128)} %param.12) | copy-start | bytes 1540
  139.5 5.3 %copy-start.2 = (f32[16,2,32]{2,1,0:T(2,128)S(1)}, f32[16,2,32]{2,1,0:T(2,128)}, u32[]{:S(2)}) copy-start(f32[16,2,32]{2,1,0:T(2,128)} %param.11) | copy-start | bytes 12292
  139.5 56.1 %all-to-all-start.2 = ((bf16[16,4,32,1024]{3,2,1,0:T(8,128)(2,1)}), bf16[16,4,32,1024]{3,2,1,0:T(8,128)(2,1)}, u32[]{:S(2)}, u32[]{:S(2)}) async-start(bf16[16,4,32,1024]{3,2,1,0:T(8,128)(2,1)} %convolution_convert_fusion.3), calls=%async_computation.2 | async-start | bytes 8388608 | tf_op jit(solution)/shard_map/all_to_all | solution.py:47
  202.1 1.3 copy-start.1
where the time goes:
time: 270 us; the launch traced here: 265 us
  blocking collectives  79.9 us (30%)
  waiting for transfers between devices  77.7 us (29%)
  local copies, waits for them, and re-layouts  74.5 us (28%)
  matrix products  19.8 us (7%)
  starting transfers between devices  10.8 us (4%)
    all_to_all x1, blocking collectives, on_device(): lax.all_to_all(outgoing, 'orb', split_axis=0, concat_axis=0, tiled=True)  79.9 us
    gather x48, local copies, waits for them, and re-layouts  56.3 us
    all_to_all x1, waiting for transfers between devices, on_device(): lax.all_to_all(projected, 'orb', split_axis=0, concat_axis=0, tiled=True)  50.8 us
    all_to_all x1, waiting for transfers between devices, on_device(): lax.all_to_all(raw_ints, 'aux', split_axis=0, concat_axis=2, tiled=True)  27 us
    unnamed x18, local copies, waits for them, and re-layouts  15.8 us
    dot_general x1, matrix products, on_device(): jnp.einsum('scpd,fd->scpf', lax.all_to_all(outgoing, 'orb', split_axis=0,...  15.3 us
    all_to_all x1, starting transfers between devices, on_device(): lax.all_to_all(raw_ints, 'aux', split_axis=0, concat_axis=2, tiled=True)  5.94 us
  transfers between devices with their start and end apart: 2, of which 2 were waited for; matrix products, arithmetic and copies ran while one was open for 4% of the time, Pallas kernels for 0%

commit v1 on v0

v1 whole, which is shorter than its diff:
```python
import functools

import jax
import jax.numpy as jnp
from jax import lax
from jax.experimental import pallas as pl
from jax.experimental.pallas import tpu as pltpu
from jax.sharding import PartitionSpec as P

MESH = pl.DeviceIdType.MESH
HOPS = (1, 3, 2)
CAP = 4
LAG = 3


def exchange_kernel(
    side_of_slot, slot_of_side, offsets, raw_ref, inv_ref, coef_ref, out_ref,
    coef, inverse, rolled, gathered, fitted_t, away, mid, last, sides, back, home,
    left, right,
    local_sem, raw_send, raw_recv, p1_send, p1_recv, p2_send, p2_recv,
    r1_send, r1_recv, r2_send, r2_recv,
):
    aux = lax.axis_index("aux")
    orb = lax.axis_index("orb")
    x, core = aux // 2, lax.rem(aux, 2)
    y, z = orb // 4, lax.rem(orb, 4)
    fit = inverse.shape[0]
    dom = fitted_t.shape[0]
    npno = coef.shape[1]
    rows = raw_ref.shape[2]

    def turned(d_first, d_second):
        dy = jnp.where(core == 0, d_first, d_second)
        dz = jnp.where(core == 0, d_second, d_first)
        return lax.rem(y + dy, 4) * 4 + lax.rem(z + dz, 4)

    def raw_peer(dx, dc):
        return lax.rem(x + dx, 4) * 2 + lax.rem(core + dc, 2)

    load_coef = pltpu.make_async_copy(coef_ref, coef, local_sem.at[0])
    load_inverse = pltpu.make_async_copy(inv_ref.at[0], inverse, local_sem.at[1])
    load_own = pltpu.make_async_copy(
        raw_ref.at[aux, 0], gathered.at[pl.ds(aux * rows, rows)], local_sem.at[2]
    )
    load_coef.start()
    load_inverse.start()
    load_own.start()

    raw_hops = [(0, 1), (1, 0), (3, 0), (1, 1), (3, 1), (2, 0), (2, 1)]
    barrier = pltpu.get_barrier_semaphore()
    for d in HOPS:
        pl.semaphore_signal(barrier, 1, device_id=(aux, turned(d, 0)), device_id_type=MESH)
        pl.semaphore_signal(barrier, 1, device_id=(aux, turned(0, d)), device_id_type=MESH)
    for hop in raw_hops:
        pl.semaphore_signal(barrier, 1, device_id=(raw_peer(*hop), orb), device_id_type=MESH)
    pl.semaphore_wait(barrier, 2 * len(HOPS) + len(raw_hops))

    raw_copies = []
    for i, hop in enumerate(raw_hops):
        peer = raw_peer(*hop)
        raw_copies.append(
            pltpu.make_async_remote_copy(
                src_ref=raw_ref.at[peer, 0],
                dst_ref=gathered.at[pl.ds(aux * rows, rows)],
                send_sem=raw_send.at[i],
                recv_sem=raw_recv.at[i],
                device_id=(peer, orb),
                device_id_type=MESH,
            )
        )
        raw_copies[-1].start()

    def stage(da, db):
        base = turned(da, db) * CAP
        for j in range(CAP):
            away[da, db, j] = coef[side_of_slot[base + j]]

    first, second, third, fourth = {}, {}, {}, {}

    def send_first(da, db):
        k = (da - 1) * 4 + db
        first[da, db] = pltpu.make_async_remote_copy(
            src_ref=away.at[da, db], dst_ref=mid.at[da - 1, db],
            send_sem=p1_send.at[k], recv_sem=p1_recv.at[k],
            device_id=(aux, turned(da, 0)), device_id_type=MESH,
        )
        first[da, db].start()

    def send_second(da, db):
        k = da * 3 + db - 1
        source = away.at[0, db] if da == 0 else mid.at[da - 1, db]
        second[da, db] = pltpu.make_async_remote_copy(
            src_ref=source, dst_ref=last.at[da, db - 1],
            send_sem=p2_send.at[k], recv_sem=p2_recv.at[k],
            device_id=(aux, turned(0, db)), device_id_type=MESH,
        )
        second[da, db].start()

    def send_third(da, db):
        k = da * 3 + db - 1
        target = home.at[0, db] if da == 0 else back.at[da - 1, db - 1]
        third[da, db] = pltpu.make_async_remote_copy(
            src_ref=sides.at[da, db], dst_ref=target,
            send_sem=r1_send.at[k], recv_sem=r1_recv.at[k],
            device_id=(aux, turned(0, 4 - db)), device_id_type=MESH,
        )
        third[da, db].start()

    def send_fourth(da, db):
        k = (da - 1) * 4 + db
        source = sides.at[da, 0] if db == 0 else back.at[da - 1, db - 1]
        fourth[da, db] = pltpu.make_async_remote_copy(
            src_ref=source, dst_ref=home.at[da, db],
            send_sem=r2_send.at[k], recv_sem=r2_recv.at[k],
            device_id=(aux, turned(4 - da, 0)), device_id_type=MESH,
        )
        fourth[da, db].start()

    load_coef.wait()
    for db in (1, 3, 2, 0):
        for da in HOPS:
            stage(da, db)
            send_first(da, db)
        if db != 0:
            stage(0, db)
            send_second(0, db)
    stage(0, 0)

    load_inverse.wait()
    own_offset = offsets[aux * 16 + orb]
    tile = 256

    def turn(n, carry):
        start = pl.multiple_of(n * tile, tile)
        to_row = lax.broadcasted_iota(jnp.int32, (tile, fit), 0) + start
        from_row = lax.broadcasted_iota(jnp.int32, (tile, fit), 1)
        hit = jnp.bitwise_and(to_row - from_row - own_offset + 2 * fit, fit - 1) == 0
        pick = jnp.where(hit, 1.0, 0.0).astype(jnp.bfloat16)
        rolled[pl.ds(start, tile), :] = jnp.dot(
            pick, inverse[...], preferred_element_type=jnp.float32
        ).astype(jnp.bfloat16)
        return carry

    lax.fori_loop(0, fit // tile, turn, 0)

    for db in HOPS:
        for da in HOPS:
            first[da, db].wait_recv()
            send_second(da, db)
    for da in HOPS:
        first[da, 0].wait_recv()

    load_own.wait()
    for copy in raw_copies:
        copy.wait_recv()

    def fit_tile(n, carry):
        start = pl.multiple_of(n * tile, tile)
        block = jnp.dot(
            rolled[...], gathered[:, pl.ds(start, tile)], preferred_element_type=jnp.float32
        ).astype(jnp.bfloat16)
        fitted_t[pl.ds(start, tile), :] = block.T
        return carry

    lax.fori_loop(0, dom // tile, fit_tile, 0)

    def project(source, target):
        def columns(n, carry):
            start = pl.multiple_of(n * tile, tile)
            lhs = source[...].reshape(CAP * npno, dom)
            block = jnp.dot(
                lhs, fitted_t[:, pl.ds(start, tile)], preferred_element_type=jnp.float32
            ).astype(jnp.bfloat16)
            target[:, :, pl.ds(start, tile)] = block.reshape(CAP, npno, tile)
            return carry

        lax.fori_loop(0, fit // tile, columns, 0)

    for da in HOPS:
        project(mid.at[da - 1, 0], sides.at[da, 0])
        send_fourth(da, 0)
    project(away.at[0, 0], home.at[0, 0])
    order = [(0, db) for db in HOPS] + [(da, db) for db in HOPS for da in HOPS]
    for i, (da, db) in enumerate(order):
        second[da, db].wait_recv()
        project(last.at[da, db - 1], sides.at[da, db])
        send_third(da, db)
        if i >= LAG and order[i - LAG][0] != 0:
            third[order[i - LAG]].wait_recv()
            send_fourth(*order[i - LAG])
    for key in order[len(order) - LAG:]:
        third[key].wait_recv()
        send_fourth(*key)
    for db in HOPS:
        third[0, db].wait_recv()
    for copy in fourth.values():
        copy.wait_recv()

    def where_home(side):
        slot = slot_of_side[side]
        p = slot // CAP
        dy = lax.rem(p // 4 + 4 - y, 4)
        dz = lax.rem(lax.rem(p, 4) + 4 - z, 4)
        da = jnp.where(core == 0, dy, dz)
        db = jnp.where(core == 0, dz, dy)
        return (da * 4 + db) * CAP + lax.rem(slot, CAP), offsets[aux * 16 + p]

    flat = home.reshape(16 * CAP, npno, fit)
    per = tile // npno
    lane = lax.broadcasted_iota(jnp.int32, (npno, fit), 1)
    for half in range(out_ref.shape[0] // per):
        for i in range(per):
            n = half * per + i
            at_0, off_0 = where_home(2 * n)
            at_1, off_1 = where_home(2 * n + 1)
            low, high = jnp.minimum(off_0, off_1), jnp.maximum(off_0, off_1)
            one = flat[at_0]
            outside = jnp.logical_and(lane >= low, lane < high)
            left[pl.ds(i * npno, npno), :] = jnp.where(outside, jnp.zeros_like(one), one)
            right[pl.ds(i * npno, npno), :] = flat[at_1]
        both = lax.dot_general(
            left[...], right[...], (((1,), (1,)), ((), ())), preferred_element_type=jnp.float32
        )
        for i in range(per):
            out_ref[half * per + i] = both[
                i * npno:(i + 1) * npno, i * npno:(i + 1) * npno
            ]

    for copy in raw_copies:
        copy.wait_send()
    for group in (first, second, third, fourth):
        for copy in group.values():
            copy.wait_send()


def on_device(raw_ints, fit_inverse, pair_orbs, pno_coef, pno_energy, occ_energy, fit_offset):
    region = lax.axis_index("aux")
    orb_count = lax.axis_size("orb")
    pairs, _, npno, dom = pno_coef.shape
    fit = fit_inverse.shape[1]
    side_count = 2 * pairs
    side_orbs = pair_orbs.reshape(side_count)
    sequence = jnp.arange(side_count, dtype=jnp.int32)
    same = side_orbs[:, None] == side_orbs[None, :]
    earlier = sequence[None, :] < sequence[:, None]
    slot_of_side = side_orbs * CAP + jnp.sum(jnp.where(same & earlier, 1, 0), axis=1)
    slots = jnp.arange(orb_count * CAP, dtype=jnp.int32)
    side_of_slot = jnp.sum(
        jnp.where(slots[:, None] == slot_of_side[None, :], sequence[None, :], 0), axis=1
    )
    bf16 = jnp.bfloat16
    vmem = pltpu.VMEM
    dma = pltpu.SemaphoreType.DMA
    smem_spec = pl.BlockSpec(memory_space=pltpu.SMEM)
    any_spec = pl.BlockSpec(memory_space=pl.ANY)
    coupling = pl.pallas_call(
        exchange_kernel,
        out_shape=jax.ShapeDtypeStruct((pairs, npno, npno), jnp.float32),
        in_specs=[smem_spec] * 3 + [any_spec] * 3,
        out_specs=pl.BlockSpec(memory_space=pltpu.VMEM),
        scratch_shapes=[
            vmem((side_count, npno, dom), bf16),
            vmem((fit, fit), bf16),
            vmem((fit, fit), bf16),
            vmem((fit, dom), bf16),
            vmem((dom, fit), bf16),
            vmem((4, 4, CAP, npno, dom), bf16),
            vmem((3, 4, CAP, npno, dom), bf16),
            vmem((4, 3, CAP, npno, dom), bf16),
            vmem((4, 4, CAP, npno, fit), bf16),
            vmem((3, 3, CAP, npno, fit), bf16),
            vmem((4, 4, CAP, npno, fit), bf16),
            vmem((256, fit), bf16),
            vmem((256, fit), bf16),
            dma((3,)), dma((7,)), dma((7,)),
            dma((12,)), dma((12,)), dma((12,)), dma((12,)),
            dma((12,)), dma((12,)), dma((12,)), dma((12,)),
        ],
        compiler_params=pltpu.CompilerParams(
            collective_id=0, has_side_effects=True, vmem_limit_bytes=56 * 2**20
        ),
        name="exchange",
    )(
        side_of_slot, slot_of_side, fit_offset,
        raw_ints, fit_inverse, pno_coef.reshape(side_count, npno, dom),
    )
    global_orb = region * orb_count + pair_orbs
    orbitals = jnp.arange(occ_energy.shape[0], dtype=jnp.int32)
    selector = global_orb[:, :, None] == orbitals[None, None, :]
    occupied = jnp.sum(jnp.where(selector, occ_energy[None, None, :], 0.0), axis=2)
    denominator = (
        pno_energy[:, 0, :, None]
        + pno_energy[:, 1, None, :]
        - occupied[:, 0, None, None]
        - occupied[:, 1, None, None]
    )
    amplitude = -coupling / denominator
    energy = jnp.sum(coupling * (2.0 * amplitude - jnp.swapaxes(amplitude, 1, 2)), axis=(1, 2))
    return (amplitude.reshape(pairs, npno * npno), energy)


def solution(mesh):
    return jax.shard_map(
        on_device,
        mesh=mesh,
        in_specs=(
            P(None, "orb", "aux", None),
            P(("aux", "orb"), None, None),
            P(("aux", "orb"), None),
            P(("aux", "orb"), None, None, None),
            P(("aux", "orb"), None, None),
            P(),
            P(),
        ),
        out_specs=(P(("aux", "orb"), None), P(("aux", "orb"))),
        check_vma=False,
    )
```

time: 270 us -> 151 us (0.56)
  the two profiles are of different devices: /device:TPU:1 before, /device:TPU:18 now
where the time goes in v1:
time: 151 us
  Pallas kernels  142 us (94%)
  other arithmetic  4.12 us (3%)
  local copies, waits for them, and re-layouts  3.77 us (2%)
    pallas_call x1, Pallas kernels, on_device(): pl.pallas_call(exchange_kernel, out_shape=jax.ShapeDtypeStruct((pairs, np...  142 us

profile of v1, /device:TPU:18, one launch (start us, length us, event | category | flops | bytes accessed | tf_op | source)
XLA Modules:
  0.0 150.7 jit_solution(16137217487854350618)
XLA Ops:
  0.6 0.7 broadcast_add_fusion
  1.3 0.8 select_reduce_fusion
  2.1 0.8 copy.18
  2.9 0.1 reshape.28
  3.0 0.2 select_reduce_fusion.2
  3.2 0.0 copy-start
  3.2 0.6 select_reduce_fusion.1.side_of_slot
  3.8 0.8 fusion.3
  4.6 0.0 copy-done
  4.6 142.1 %exchange.1 = f32[16,32,32]{2,1,0:T(8,128)} custom-call(s32[64]{0:T(128)} %select_reduce_fusion.1.side_of_slot, s32[32]{0:T(128)} %copy-done, s32[128]{0:T(128)} %offsets.1, bf16[8,1,128,1536]{3,2,1,0:T(8,128)(2,1)} %raw_ref.1, bf16[1,1024,1024]{2,1,0:T(8,128)(2,1)} %inv_ref.1, bf16[32,32,1536]{2,1,0:T(8,128)(2,1)} %bitcast.13), custom_call_target="tpu_custom_call" | custom-call | tf_op jit(solution)/shard_map/exchange/pallas_call | solution.py:256
  146.7 1.1 copy.19
  147.8 0.2 broadcast_multiply_fusion
  148.0 0.1 copy.21
  148.1 1.7 %fusion.1 = f32[16]{0:T(128)} fusion(f32[16,32,32]{2,1,0:T(8,128)} %exchange.1, f32[16,32,32]{2,1,0:T(8,128)S(1)} %copy.21, f32[16,32,32]{1,2,0:T(8,128)S(1)} %get-tuple-element.3), kind=kLoop, calls=%fused_computation.2 | loop fusion | flops 49136 | bytes 196672 | tf_op jit(solution)/shard_map/reduce_sum | solution.py:298
  149.8 0.1 copy.20
  149.9 0.8 reshape.30
  (2 shorter events, 0.0 us)
Async XLA Ops:
  3.2 1.4 copy-start

commit v2 on v1

--- a/solution.py
+++ b/solution.py
@@ -1,5 +1,3 @@
-import functools
-
 import jax
 import jax.numpy as jnp
 from jax import lax
@@ -9,14 +7,16 @@
 
 MESH = pl.DeviceIdType.MESH
 HOPS = (1, 3, 2)
+RAW_HOPS = ((0, 1), (1, 0), (3, 0), (1, 1), (3, 1), (2, 0), (2, 1))
 CAP = 4
 LAG = 3
+EXACT = lax.Precision.HIGHEST
 
 
 def exchange_kernel(
-    side_of_slot, slot_of_side, offsets, raw_ref, inv_ref, coef_ref, out_ref,
+    pair_orbs, offsets, occupied, levels, raw_ref, inv_ref, coef_ref, out_ref, energy_ref,
     coef, inverse, rolled, gathered, fitted_t, away, mid, last, sides, back, home,
-    left, right,
+    left, right, gap, spread, table, lookup,
     local_sem, raw_send, raw_recv, p1_send, p1_recv, p2_send, p2_recv,
     r1_send, r1_recv, r2_send, r2_recv,
 ):
@@ -26,7 +26,8 @@
     y, z = orb // 4, lax.rem(orb, 4)
     fit = inverse.shape[0]
     dom = fitted_t.shape[0]
-    npno = coef.shape[1]
+    side_count, npno, _ = coef.shape
+    pairs = side_count // 2
     rows = raw_ref.shape[2]
 
     def turned(d_first, d_second):
@@ -46,17 +47,39 @@
     load_inverse.start()
     load_own.start()
 
-    raw_hops = [(0, 1), (1, 0), (3, 0), (1, 1), (3, 1), (2, 0), (2, 1)]
     barrier = pltpu.get_barrier_semaphore()
     for d in HOPS:
         pl.semaphore_signal(barrier, 1, device_id=(aux, turned(d, 0)), device_id_type=MESH)
         pl.semaphore_signal(barrier, 1, device_id=(aux, turned(0, d)), device_id_type=MESH)
-    for hop in raw_hops:
+    for hop in RAW_HOPS:
         pl.semaphore_signal(barrier, 1, device_id=(raw_peer(*hop), orb), device_id_type=MESH)
-    pl.semaphore_wait(barrier, 2 * len(HOPS) + len(raw_hops))
-
+
+    lane = lax.broadcasted_iota(jnp.int32, (8, 128), 1)
+    slot_orb, slot_place = lane // CAP, jnp.bitwise_and(lane, CAP - 1)
+    zero = jnp.zeros((8, 128), jnp.int32)
+    in_slot, seen, own_orb, place = zero, zero, zero, zero
+    for i in range(side_count):
+        name = pair_orbs[i // 2, i % 2]
+        match = slot_orb == name
+        in_slot = jnp.where(jnp.logical_and(match, seen == slot_place), i, in_slot)
+        seen = seen + jnp.where(match, 1, 0)
+        own_orb = jnp.where(lane == i, name, own_orb)
+    for i in range(side_count):
+        name = pair_orbs[i // 2, i % 2]
+        place = place + jnp.where(jnp.logical_and(own_orb == name, lane > i), 1, 0)
+    dy = jnp.bitwise_and(own_orb // 4 + 4 - y, 3)
+    dz = jnp.bitwise_and(own_orb + 4 - z, 3)
+    along = jnp.where(core == 0, dy, dz)
+    across = jnp.where(core == 0, dz, dy)
+    home_slot = (along * 4 + across) * CAP + jnp.minimum(place, CAP - 1)
+    first_row = lax.broadcasted_iota(jnp.int32, (8, 128), 0) == 0
+    table[...] = jnp.where(first_row, in_slot, home_slot)
+    load_table = pltpu.make_async_copy(table, lookup, local_sem.at[3])
+    load_table.start()
+
+    pl.semaphore_wait(barrier, 2 * len(HOPS) + len(RAW_HOPS))
     raw_copies = []
-    for i, hop in enumerate(raw_hops):
+    for i, hop in enumerate(RAW_HOPS):
         peer = raw_peer(*hop)
         raw_copies.append(
             pltpu.make_async_remote_copy(
@@ -73,7 +96,7 @@
     def stage(da, db):
         base = turned(da, db) * CAP
         for j in range(CAP):
-            away[da, db, j] = coef[side_of_slot[base + j]]
+            away[da, db, j] = coef[lookup[0, base + j]]
 
     first, second, third, fourth = {}, {}, {}, {}
 
@@ -117,6 +140,7 @@
         fourth[da, db].start()
 
     load_coef.wait()
+    load_table.wait()
     for db in (1, 3, 2, 0):
         for da in HOPS:
             stage(da, db)
@@ -125,6 +149,36 @@
             stage(0, db)
             send_second(0, db)
     stage(0, 0)
+
+    wide = pairs * npno
+    of_lane = lax.broadcasted_iota(jnp.int32, (pairs, wide), 1) // npno
+    in_pair = of_lane == lax.broadcasted_iota(jnp.int32, (pairs, wide), 0)
+    repeat = jnp.where(
+        lax.broadcasted_iota(jnp.int32, (npno, wide), 0)
+        == jnp.bitwise_and(lax.broadcasted_iota(jnp.int32, (npno, wide), 1), npno - 1),
+        1.0, 0.0,
+    )
+    choose = jnp.where(in_pair, 1.0, 0.0)
+    pair_lane = lax.broadcasted_iota(jnp.int32, (1, wide), 1) // npno
+    filled = jnp.zeros((1, wide), jnp.float32)
+    for n in range(pairs):
+        both_occupied = (
+            occupied[aux * 16 + pair_orbs[n, 0]] + occupied[aux * 16 + pair_orbs[n, 1]]
+        )
+        filled = jnp.where(pair_lane == n, both_occupied, filled)
+    down, along_lanes = [], []
+    for k in range(2):
+        level = levels[:, k, :]
+        down.append(
+            lax.dot_general(
+                level, choose, (((0,), (0,)), ((), ())), precision=EXACT,
+                preferred_element_type=jnp.float32,
+            )
+        )
+        every = jnp.dot(level, repeat, precision=EXACT, preferred_element_type=jnp.float32)
+        along_lanes.append(jnp.sum(jnp.where(in_pair, every, 0.0), axis=0, keepdims=True))
+    gap[0] = down[0] + along_lanes[1] - filled
+    gap[1] = down[1] + along_lanes[0] - filled
 
     load_inverse.wait()
     own_offset = offsets[aux * 16 + orb]
@@ -196,35 +250,65 @@
     for copy in fourth.values():
         copy.wait_recv()
 
-    def where_home(side):
-        slot = slot_of_side[side]
-        p = slot // CAP
-        dy = lax.rem(p // 4 + 4 - y, 4)
-        dz = lax.rem(lax.rem(p, 4) + 4 - z, 4)
-        da = jnp.where(core == 0, dy, dz)
-        db = jnp.where(core == 0, dz, dy)
-        return (da * 4 + db) * CAP + lax.rem(slot, CAP), offsets[aux * 16 + p]
-
     flat = home.reshape(16 * CAP, npno, fit)
     per = tile // npno
-    lane = lax.broadcasted_iota(jnp.int32, (npno, fit), 1)
-    for half in range(out_ref.shape[0] // per):
+    lanes = 128
+    packed = lanes // npno
+    fit_lane = lax.broadcasted_iota(jnp.int32, (npno, fit), 1)
+    block_of = lax.broadcasted_iota(jnp.int32, (npno, lanes), 1) // npno
+    contract = (((1,), (1,)), ((), ()))
+    energies = jnp.zeros((1, lanes), jnp.float32)
+    one_lane = lax.broadcasted_iota(jnp.int32, (1, lanes), 1)
+    for half in range(pairs // per):
         for i in range(per):
             n = half * per + i
-            at_0, off_0 = where_home(2 * n)
-            at_1, off_1 = where_home(2 * n + 1)
+            off_0 = offsets[aux * 16 + pair_orbs[n, 0]]
+            off_1 = offsets[aux * 16 + pair_orbs[n, 1]]
             low, high = jnp.minimum(off_0, off_1), jnp.maximum(off_0, off_1)
-            one = flat[at_0]
-            outside = jnp.logical_and(lane >= low, lane < high)
+            one = flat[lookup[1, 2 * n]]
+            outside = jnp.logical_and(fit_lane >= low, fit_lane < high)
             left[pl.ds(i * npno, npno), :] = jnp.where(outside, jnp.zeros_like(one), one)
-            right[pl.ds(i * npno, npno), :] = flat[at_1]
-        both = lax.dot_general(
-            left[...], right[...], (((1,), (1,)), ((), ())), preferred_element_type=jnp.float32
-        )
-        for i in range(per):
-            out_ref[half * per + i] = both[
-                i * npno:(i + 1) * npno, i * npno:(i + 1) * npno
-            ]
+            right[pl.ds(i * npno, npno), :] = flat[lookup[1, 2 * n + 1]]
+        ahead = lax.dot_general(
+            left[...], right[...], contract, preferred_element_type=jnp.float32
+        )
+        behind = lax.dot_general(
+            right[...], left[...], contract, preferred_element_type=jnp.float32
+        )
+        for part in range(per // packed):
+            forward = jnp.zeros((npno, lanes), jnp.float32)
+            swapped = jnp.zeros((npno, lanes), jnp.float32)
+            for i in range(packed):
+                at = (part * packed + i) * npno
+                here = block_of == i
+                cut = slice(part * lanes, (part + 1) * lanes)
+                forward = jnp.where(here, ahead[at:at + npno, cut], forward)
+                swapped = jnp.where(here, behind[at:at + npno, cut], swapped)
+            first_pair = half * per + part * packed
+            span = pl.ds(first_pair * npno, lanes)
+            amplitude = -forward / gap[0, :, span]
+            mirrored = -swapped / gap[1, :, span]
+            share = jnp.sum(
+                forward * (2.0 * amplitude - mirrored), axis=0, keepdims=True
+            )
+            for shift in (1, 2, 4, 8, 16):
+                share = share + pltpu.roll(share, lanes - shift, 1)
+            for i in range(packed):
+                n = first_pair + i
+                energies = jnp.where(
+                    one_lane == n, pltpu.roll(share, (n - i * npno) % lanes, 1), energies
+                )
+            spread[...] = amplitude
+            strided = [spread[pl.ds(u, npno // packed, stride=packed), :] for u in range(packed)]
+            for i in range(packed):
+                line = jnp.zeros((npno // packed, lanes), jnp.float32)
+                for u in range(packed):
+                    moved = pltpu.roll(strided[u], ((u - i) * npno) % lanes, 1)
+                    line = jnp.where(block_of[:npno // packed] == u, moved, line)
+                n = first_pair + i
+                for t in range(npno // packed):
+                    out_ref[n:n + 1, t * lanes:(t + 1) * lanes] = line[t:t + 1]
+    energy_ref[...] = energies
 
     for copy in raw_copies:
         copy.wait_send()
@@ -234,32 +318,25 @@
 
 
 def on_device(raw_ints, fit_inverse, pair_orbs, pno_coef, pno_energy, occ_energy, fit_offset):
-    region = lax.axis_index("aux")
-    orb_count = lax.axis_size("orb")
     pairs, _, npno, dom = pno_coef.shape
     fit = fit_inverse.shape[1]
-    side_count = 2 * pairs
-    side_orbs = pair_orbs.reshape(side_count)
-    sequence = jnp.arange(side_count, dtype=jnp.int32)
-    same = side_orbs[:, None] == side_orbs[None, :]
-    earlier = sequence[None, :] < sequence[:, None]
-    slot_of_side = side_orbs * CAP + jnp.sum(jnp.where(same & earlier, 1, 0), axis=1)
-    slots = jnp.arange(orb_count * CAP, dtype=jnp.int32)
-    side_of_slot = jnp.sum(
-        jnp.where(slots[:, None] == slot_of_side[None, :], sequence[None, :], 0), axis=1
-    )
     bf16 = jnp.bfloat16
+    f32 = jnp.float32
     vmem = pltpu.VMEM
     dma = pltpu.SemaphoreType.DMA
     smem_spec = pl.BlockSpec(memory_space=pltpu.SMEM)
+    vmem_spec = pl.BlockSpec(memory_space=pltpu.VMEM)
     any_spec = pl.BlockSpec(memory_space=pl.ANY)
-    coupling = pl.pallas_call(
+    amplitude, energy = pl.pallas_call(
         exchange_kernel,
-        out_shape=jax.ShapeDtypeStruct((pairs, npno, npno), jnp.float32),
-        in_specs=[smem_spec] * 3 + [any_spec] * 3,
-        out_specs=pl.BlockSpec(memory_space=pltpu.VMEM),
+        out_shape=(
+            jax.ShapeDtypeStruct((pairs, npno * npno), f32),
+            jax.ShapeDtypeStruct((1, 128), f32),
+        ),
+        in_specs=[smem_spec] * 3 + [vmem_spec] + [any_spec] * 3,
+        out_specs=(vmem_spec, vmem_spec),
         scratch_shapes=[
-            vmem((side_count, npno, dom), bf16),
+            vmem((2 * pairs, npno, dom), bf16),
             vmem((fit, fit), bf16),
             vmem((fit, fit), bf16),
             vmem((fit, dom), bf16),
@@ -272,7 +349,11 @@
             vmem((4, 4, CAP, npno, fit), bf16),
             vmem((256, fit), bf16),
             vmem((256, fit), bf16),
-            dma((3,)), dma((7,)), dma((7,)),
+            vmem((2, npno, pairs * npno), f32),
+            vmem((npno, 128), f32),
+            vmem((8, 128), jnp.int32),
+            pltpu.SMEM((8, 128), jnp.int32),
+            dma((4,)), dma((7,)), dma((7,)),
             dma((12,)), dma((12,)), dma((12,)), dma((12,)),
             dma((12,)), dma((12,)), dma((12,)), dma((12,)),
         ],
@@ -281,22 +362,10 @@
         ),
         name="exchange",
     )(
-        side_of_slot, slot_of_side, fit_offset,
-        raw_ints, fit_inverse, pno_coef.reshape(side_count, npno, dom),
+        pair_orbs, fit_offset, occ_energy, pno_energy,
+        raw_ints, fit_inverse, pno_coef.reshape(2 * pairs, npno, dom),
     )
-    global_orb = region * orb_count + pair_orbs
-    orbitals = jnp.arange(occ_energy.shape[0], dtype=jnp.int32)
-    selector = global_orb[:, :, None] == orbitals[None, None, :]
-    occupied = jnp.sum(jnp.where(selector, occ_energy[None, None, :], 0.0), axis=2)
-    denominator = (
-        pno_energy[:, 0, :, None]
-        + pno_energy[:, 1, None, :]
-        - occupied[:, 0, None, None]
-        - occupied[:, 1, None, None]
-    )
-    amplitude = -coupling / denominator
-    energy = jnp.sum(coupling * (2.0 * amplitude - jnp.swapaxes(amplitude, 1, 2)), axis=(1, 2))
-    return (amplitude.reshape(pairs, npno * npno), energy)
+    return amplitude, energy[0, :pairs]
 
 
 def solution(mesh):

time: 151 us -> 147 us (0.974)
  other arithmetic: 4.12 us -> 0 us
    reduce_sum x4 -> x0, other arithmetic: 3.25 us -> none  [the longest x1 1.67 us: on_device(): jnp.sum(coupling * (2.0 * amplitude - jnp.swapaxes(amplitude, 1, 2)), axi...]
    unnamed x3 -> x2, local copies, waits for them, and re-layouts: 0.76 us -> 2.83 us
where the time goes in v2:
time: 147 us
  Pallas kernels  142 us (97%)
  local copies, waits for them, and re-layouts  3.95 us (3%)
    pallas_call x1, Pallas kernels, on_device(): pl.pallas_call(exchange_kernel, out_shape=(jax.ShapeDtypeStruct((pairs, n...  142 us

profile of v2, /device:TPU:18, one launch (start us, length us, event | category | flops | bytes accessed | tf_op | source)
XLA Modules:
  0.0 146.6 jit_solution(8009734333191257328)
XLA Ops:
  0.6 1.4 copy.9.pair_orbs
  2.0 142.0 %exchange.1 = (f32[16,1024]{1,0:T(8,128)}, f32[1,128]{1,0:T(1,128)}) custom-call(s32[16,2]{1,0:T(8,128)} %copy.9.pair_orbs, s32[128]{0:T(128)} %offsets.1, f32[128]{0:T(128)} %occupied.1, f32[16,2,32]{2,1,0:T(2,128)} %levels.1, bf16[8,1,128,1536]{3,2,1,0:T(8,128)(2,1)} %raw_ref.1, bf16[1,1024,1024]{2,1,0:T(8,128)(2,1)} %inv_ref.1, bf16[32,32,1536]{2,1,0:T(8,128)(2,1)} %bitcast.3), custom_call_target="tpu_custom_call" | custom-call | tf_op jit(solution)/shard_map/exchange/pallas_call | solution.py:330
  144.0 1.1 slice_bitcast_fusion
  145.1 1.5 %copy.11 = f32[16,1024]{1,0:T(8,128)} copy(f32[16,1024]{1,0:T(8,128)} %get-tuple-element.8) | data formatting | bytes 131072

commit v3 on v2

--- a/solution.py
+++ b/solution.py
@@ -9,17 +9,24 @@
 HOPS = (1, 3, 2)
 RAW_HOPS = ((0, 1), (1, 0), (3, 0), (1, 1), (3, 1), (2, 0), (2, 1))
 CAP = 4
-LAG = 3
+ROW = 12
+SENDS = {8: 1, 11: 3}
 EXACT = lax.Precision.HIGHEST
 
 
 def exchange_kernel(
-    pair_orbs, offsets, occupied, levels, raw_ref, inv_ref, coef_ref, out_ref, energy_ref,
-    coef, inverse, rolled, gathered, fitted_t, away, mid, last, sides, back, home,
-    left, right, gap, spread, table, lookup,
+    pair_orbs, offsets, occupied, levels, raw_ref, inv_ref, coef_ref,
+    out_ref, energy_ref, crowded_ref,
+    coef, inverse, rolled, gathered, fitted_t, packed_out, mid_1, mid_2, mid_3, away, last,
+    sides, back_1, back_2, back_3, packed_back, home,
+    left, right, gap, spread, table, note, notes, flags_out, flags_across, flags_aux,
+    lookup, notices,
     local_sem, raw_send, raw_recv, p1_send, p1_recv, p2_send, p2_recv,
-    r1_send, r1_recv, r2_send, r2_recv,
+    r1_send, r1_recv, r2_send, r2_recv, note_send, note_recv, note_sem,
+    across_send, across_recv, aux_send, aux_recv,
 ):
+    mid = {1: mid_1, 2: mid_2, 3: mid_3}
+    back = {1: back_1, 2: back_2, 3: back_3}
     aux = lax.axis_index("aux")
     orb = lax.axis_index("orb")
     x, core = aux // 2, lax.rem(aux, 2)
@@ -54,26 +61,68 @@
     for hop in RAW_HOPS:
         pl.semaphore_signal(barrier, 1, device_id=(raw_peer(*hop), orb), device_id_type=MESH)
 
+    own_along = jnp.where(core == 0, y, z)
+    own_across = jnp.where(core == 0, z, y)
+
+    def row_of(p):
+        return jnp.where(core == 0, p // 4, jnp.bitwise_and(p, 3))
+
+    def place_in_row(p):
+        return jnp.where(core == 0, jnp.bitwise_and(p, 3), p // 4)
+
     lane = lax.broadcasted_iota(jnp.int32, (8, 128), 1)
     slot_orb, slot_place = lane // CAP, jnp.bitwise_and(lane, CAP - 1)
+    slot_row = row_of(slot_orb)
+    list_row, list_place = lane // 16, jnp.bitwise_and(lane, 15)
     zero = jnp.zeros((8, 128), jnp.int32)
-    in_slot, seen, own_orb, place = zero, zero, zero, zero
+    in_slot, in_list, list_orb, slot_list = zero, zero, zero, zero
+    seen, seen_row, seen_list, own_orb = zero, zero, zero, zero
     for i in range(side_count):
-        name = pair_orbs[i // 2, i % 2]
+        name = pair_orbs[i % 2, i // 2]
+        row = row_of(name)
         match = slot_orb == name
-        in_slot = jnp.where(jnp.logical_and(match, seen == slot_place), i, in_slot)
+        hit = jnp.logical_and(match, seen == slot_place)
+        in_slot = jnp.where(hit, i, in_slot)
+        slot_list = jnp.where(hit, seen_row, slot_list)
         seen = seen + jnp.where(match, 1, 0)
+        seen_row = seen_row + jnp.where(slot_row == row, 1, 0)
+        match = list_row == row
+        hit = jnp.logical_and(match, seen_list == list_place)
+        in_list = jnp.where(hit, i, in_list)
+        list_orb = jnp.where(hit, name, list_orb)
+        seen_list = seen_list + jnp.where(match, 1, 0)
         own_orb = jnp.where(lane == i, name, own_orb)
+    own_row = row_of(own_orb)
+    side_place, side_list, list_spot = zero, zero, zero
     for i in range(side_count):
-        name = pair_orbs[i // 2, i % 2]
-        place = place + jnp.where(jnp.logical_and(own_orb == name, lane > i), 1, 0)
-    dy = jnp.bitwise_and(own_orb // 4 + 4 - y, 3)
-    dz = jnp.bitwise_and(own_orb + 4 - z, 3)
-    along = jnp.where(core == 0, dy, dz)
-    across = jnp.where(core == 0, dz, dy)
-    home_slot = (along * 4 + across) * CAP + jnp.minimum(place, CAP - 1)
-    first_row = lax.broadcasted_iota(jnp.int32, (8, 128), 0) == 0
-    table[...] = jnp.where(first_row, in_slot, home_slot)
+        name = pair_orbs[i % 2, i // 2]
+        after = lane > i
+        side_place = side_place + jnp.where(jnp.logical_and(own_orb == name, after), 1, 0)
+        side_list = side_list + jnp.where(
+            jnp.logical_and(own_row == row_of(name), after), 1, 0
+        )
+        list_spot = list_spot + jnp.where(
+            jnp.logical_and(list_orb == name, in_list > i), 1, 0
+        )
+    along = jnp.bitwise_and(own_row + 4 - own_along, 3)
+    across = jnp.bitwise_and(place_in_row(own_orb) + 4 - own_across, 3)
+    home_slot = jnp.where(
+        along == 0,
+        across * CAP + jnp.minimum(side_place, CAP - 1),
+        4 * CAP + (along - 1) * ROW + jnp.minimum(side_list, ROW - 1),
+    )
+    list_slot = (
+        jnp.bitwise_and(place_in_row(list_orb) + 4 - own_across, 3) * CAP
+        + jnp.minimum(list_spot, CAP - 1)
+    )
+    crowded = jnp.max(jnp.where(jnp.logical_and(list_row < 4, seen_list > ROW), 1, 0))
+    row_at = lax.broadcasted_iota(jnp.int32, (8, 128), 0)
+    table[...] = jnp.where(row_at == 0, in_slot, jnp.where(row_at == 1, home_slot, in_list))
+    note[...] = jnp.where(
+        row_at == 0,
+        jnp.minimum(slot_list, ROW - 1),
+        jnp.where(row_at == 1, list_slot, crowded),
+    )
     load_table = pltpu.make_async_copy(table, lookup, local_sem.at[3])
     load_table.start()
 
@@ -93,27 +142,28 @@
         )
         raw_copies[-1].start()
 
-    def stage(da, db):
-        base = turned(da, db) * CAP
-        for j in range(CAP):
-            away[da, db, j] = coef[lookup[0, base + j]]
-
-    first, second, third, fourth = {}, {}, {}, {}
-
-    def send_first(da, db):
-        k = (da - 1) * 4 + db
-        first[da, db] = pltpu.make_async_remote_copy(
-            src_ref=away.at[da, db], dst_ref=mid.at[da - 1, db],
-            send_sem=p1_send.at[k], recv_sem=p1_recv.at[k],
+    told, first, second, third, fourth = {}, {}, {}, {}, {}
+
+    def tell(da):
+        told[da] = pltpu.make_async_remote_copy(
+            src_ref=note, dst_ref=notes.at[da - 1],
+            send_sem=note_send.at[da - 1], recv_sem=note_recv.at[da - 1],
             device_id=(aux, turned(da, 0)), device_id_type=MESH,
         )
-        first[da, db].start()
+        told[da].start()
+
+    def send_first(da):
+        first[da] = pltpu.make_async_remote_copy(
+            src_ref=packed_out.at[da - 1], dst_ref=mid[da],
+            send_sem=p1_send.at[da - 1], recv_sem=p1_recv.at[da - 1],
+            device_id=(aux, turned(da, 0)), device_id_type=MESH,
+        )
+        first[da].start()
 
     def send_second(da, db):
         k = da * 3 + db - 1
-        source = away.at[0, db] if da == 0 else mid.at[da - 1, db]
         second[da, db] = pltpu.make_async_remote_copy(
-            src_ref=source, dst_ref=last.at[da, db - 1],
+            src_ref=away.at[da, db], dst_ref=last.at[da, db - 1],
             send_sem=p2_send.at[k], recv_sem=p2_recv.at[k],
             device_id=(aux, turned(0, db)), device_id_type=MESH,
         )
@@ -121,34 +171,44 @@
 
     def send_third(da, db):
         k = da * 3 + db - 1
-        target = home.at[0, db] if da == 0 else back.at[da - 1, db - 1]
+        spots = pl.ds(db * CAP, CAP)
         third[da, db] = pltpu.make_async_remote_copy(
-            src_ref=sides.at[da, db], dst_ref=target,
+            src_ref=sides.at[da, db - 1],
+            dst_ref=home.at[spots] if da == 0 else back[da].at[spots],
             send_sem=r1_send.at[k], recv_sem=r1_recv.at[k],
             device_id=(aux, turned(0, 4 - db)), device_id_type=MESH,
         )
         third[da, db].start()
 
-    def send_fourth(da, db):
-        k = (da - 1) * 4 + db
-        source = sides.at[da, 0] if db == 0 else back.at[da - 1, db - 1]
-        fourth[da, db] = pltpu.make_async_remote_copy(
-            src_ref=source, dst_ref=home.at[da, db],
-            send_sem=r2_send.at[k], recv_sem=r2_recv.at[k],
+    def send_fourth(da):
+        for db in HOPS:
+            third[da, db].wait_recv()
+        at = (own_along * 16)
+        for q in range(ROW):
+            packed_back[da - 1, q] = back[da][notices[da - 1, 1, at + q]]
+        fourth[da] = pltpu.make_async_remote_copy(
+            src_ref=packed_back.at[da - 1],
+            dst_ref=home.at[pl.ds(4 * CAP + (da - 1) * ROW, ROW)],
+            send_sem=r2_send.at[da - 1], recv_sem=r2_recv.at[da - 1],
             device_id=(aux, turned(4 - da, 0)), device_id_type=MESH,
         )
-        fourth[da, db].start()
-
+        fourth[da].start()
+
+    for da in HOPS:
+        tell(da)
     load_coef.wait()
     load_table.wait()
+    for da in HOPS:
+        to_row = jnp.bitwise_and(own_along + da, 3) * 16
+        for q in range(ROW):
+            packed_out[da - 1, q] = coef[lookup[2, to_row + q]]
+        send_first(da)
     for db in (1, 3, 2, 0):
-        for da in HOPS:
-            stage(da, db)
-            send_first(da, db)
+        base = turned(0, db) * CAP
+        for j in range(CAP):
+            away[0, db, j] = coef[lookup[0, base + j]]
         if db != 0:
-            stage(0, db)
             send_second(0, db)
-    stage(0, 0)
 
     wide = pairs * npno
     of_lane = lax.broadcasted_iota(jnp.int32, (pairs, wide), 1) // npno
@@ -163,7 +223,7 @@
     filled = jnp.zeros((1, wide), jnp.float32)
     for n in range(pairs):
         both_occupied = (
-            occupied[aux * 16 + pair_orbs[n, 0]] + occupied[aux * 16 + pair_orbs[n, 1]]
+            occupied[aux * 16 + pair_orbs[0, n]] + occupied[aux * 16 + pair_orbs[1, n]]
         )
         filled = jnp.where(pair_lane == n, both_occupied, filled)
     down, along_lanes = [], []
@@ -197,12 +257,54 @@
 
     lax.fori_loop(0, fit // tile, turn, 0)
 
+    unread = []
+    for da in HOPS:
+        told[da].wait_recv()
+        unread.append(
+            pltpu.make_async_copy(notes.at[da - 1], notices.at[da - 1], note_sem.at[da - 1])
+        )
+        unread[-1].start()
+    flags_out[0] = jnp.maximum(
+        jnp.maximum(notes[0], notes[1]), jnp.maximum(notes[2], note[...])
+    )
+    flag_copies = []
     for db in HOPS:
-        for da in HOPS:
-            first[da, db].wait_recv()
-            send_second(da, db)
+        flag_copies.append(
+            pltpu.make_async_remote_copy(
+                src_ref=flags_out.at[0], dst_ref=flags_across.at[db - 1],
+                send_sem=across_send.at[db - 1], recv_sem=across_recv.at[db - 1],
+                device_id=(aux, turned(0, db)), device_id_type=MESH,
+            )
+        )
+        flag_copies[-1].start()
+    for copy in unread:
+        copy.wait()
+
     for da in HOPS:
-        first[da, 0].wait_recv()
+        first[da].wait_recv()
+        for db in (1, 3, 2, 0):
+            base = turned(0, db) * CAP
+            for j in range(CAP):
+                away[da, db, j] = mid[da][notices[da - 1, 0, base + j]]
+            if db != 0:
+                send_second(da, db)
+
+    for copy in flag_copies:
+        copy.wait()
+    flags_out[1] = jnp.maximum(
+        jnp.maximum(flags_across[0], flags_across[1]),
+        jnp.maximum(flags_across[2], flags_out[0]),
+    )
+    last_flags = []
+    for i, hop in enumerate(RAW_HOPS):
+        last_flags.append(
+            pltpu.make_async_remote_copy(
+                src_ref=flags_out.at[1], dst_ref=flags_aux.at[i],
+                send_sem=aux_send.at[i], recv_sem=aux_recv.at[i],
+                device_id=(raw_peer(*hop), orb), device_id_type=MESH,
+            )
+        )
+        last_flags[-1].start()
 
     load_own.wait()
     for copy in raw_copies:
@@ -231,26 +333,21 @@
         lax.fori_loop(0, fit // tile, columns, 0)
 
     for da in HOPS:
-        project(mid.at[da - 1, 0], sides.at[da, 0])
-        send_fourth(da, 0)
-    project(away.at[0, 0], home.at[0, 0])
-    order = [(0, db) for db in HOPS] + [(da, db) for db in HOPS for da in HOPS]
+        project(away.at[da, 0], back[da].at[pl.ds(0, CAP)])
+    project(away.at[0, 0], home.at[pl.ds(0, CAP)])
+    order = [(da, db) for da in (0, 1, 3, 2) for db in HOPS]
     for i, (da, db) in enumerate(order):
         second[da, db].wait_recv()
-        project(last.at[da, db - 1], sides.at[da, db])
+        project(last.at[da, db - 1], sides.at[da, db - 1])
         send_third(da, db)
-        if i >= LAG and order[i - LAG][0] != 0:
-            third[order[i - LAG]].wait_recv()
-            send_fourth(*order[i - LAG])
-    for key in order[len(order) - LAG:]:
-        third[key].wait_recv()
-        send_fourth(*key)
+        if i in SENDS:
+            send_fourth(SENDS[i])
+    send_fourth(2)
     for db in HOPS:
         third[0, db].wait_recv()
-    for copy in fourth.values():
-        copy.wait_recv()
-
-    flat = home.reshape(16 * CAP, npno, fit)
+    for da in HOPS:
+        fourth[da].wait_recv()
+
     per = tile // npno
     lanes = 128
     packed = lanes // npno
@@ -262,13 +359,13 @@
     for half in range(pairs // per):
         for i in range(per):
             n = half * per + i
-            off_0 = offsets[aux * 16 + pair_orbs[n, 0]]
-            off_1 = offsets[aux * 16 + pair_orbs[n, 1]]
+            off_0 = offsets[aux * 16 + pair_orbs[0, n]]
+            off_1 = offsets[aux * 16 + pair_orbs[1, n]]
             low, high = jnp.minimum(off_0, off_1), jnp.maximum(off_0, off_1)
-            one = flat[lookup[1, 2 * n]]
+            one = home[lookup[1, 2 * n]]
             outside = jnp.logical_and(fit_lane >= low, fit_lane < high)
             left[pl.ds(i * npno, npno), :] = jnp.where(outside, jnp.zeros_like(one), one)
-            right[pl.ds(i * npno, npno), :] = flat[lookup[1, 2 * n + 1]]
+            right[pl.ds(i * npno, npno), :] = home[lookup[1, 2 * n + 1]]
         ahead = lax.dot_general(
             left[...], right[...], contract, preferred_element_type=jnp.float32
         )
@@ -309,12 +406,87 @@
                 for t in range(npno // packed):
                     out_ref[n:n + 1, t * lanes:(t + 1) * lanes] = line[t:t + 1]
     energy_ref[...] = energies
+    every_flag = flags_out[1]
+    for i, copy in enumerate(last_flags):
+        copy.wait()
+        every_flag = jnp.maximum(every_flag, flags_aux[i])
+    crowded_ref[...] = every_flag
 
     for copy in raw_copies:
         copy.wait_send()
-    for group in (first, second, third, fourth):
+    for group in (told, first, second, third, fourth):
         for copy in group.values():
             copy.wait_send()
+
+
+def align_rows(shifted_in, begin_at):
+    return lax.dynamic_slice_in_dim(shifted_in, begin_at, shifted_in.shape[1] * 2 // 3, 1)
+
+
+def spread_out(raw_ints, fit_inverse, pair_orbs, pno_coef, pno_energy, occ_energy, fit_offset):
+    orb_count = lax.axis_size("orb")
+    region = lax.axis_index("aux")
+    inverse = fit_inverse[0]
+    gathered = lax.all_to_all(raw_ints, "aux", split_axis=0, concat_axis=2, tiled=True)
+    fitted = jnp.dot(inverse, gathered[0, 0], preferred_element_type=jnp.float32).astype(
+        jnp.bfloat16
+    )
+    fit_rows = fitted.shape[0]
+    pair_count = pair_orbs.shape[0]
+    pno_count = pno_coef.shape[2]
+    dom_count = pno_coef.shape[3]
+    side_count = 2 * pair_count
+    capacity = max(2, 4 * pair_count // orb_count)
+    slot_count = orb_count * capacity
+    side_orbs = pair_orbs.reshape(side_count)
+    matches = side_orbs[:, None] == side_orbs[None, :]
+    sequence = jnp.arange(side_count, dtype=jnp.int32)
+    earlier = sequence[None, :] < sequence[:, None]
+    position = jnp.sum(jnp.where(matches & earlier, 1, 0), axis=1)
+    slot_index = side_orbs * capacity + position
+    placing = jnp.where(
+        slot_index[None, :] == jnp.arange(slot_count, dtype=jnp.int32)[:, None], 1.0, 0.0
+    ).astype(jnp.bfloat16)
+    outgoing = jnp.dot(
+        placing,
+        pno_coef.reshape(side_count, pno_count * dom_count),
+        preferred_element_type=jnp.float32,
+    ).astype(jnp.bfloat16)
+    outgoing = outgoing.reshape(orb_count, capacity, pno_count, dom_count)
+    projected = jnp.einsum(
+        "scpd,fd->scpf",
+        lax.all_to_all(outgoing, "orb", split_axis=0, concat_axis=0, tiled=True),
+        fitted,
+        preferred_element_type=jnp.float32,
+    ).astype(jnp.bfloat16)
+    returned = lax.all_to_all(projected, "orb", split_axis=0, concat_axis=0, tiled=True)
+    side_blocks = jnp.dot(
+        placing.T,
+        returned.reshape(slot_count, pno_count * fit_rows),
+        preferred_element_type=jnp.float32,
+    ).astype(jnp.bfloat16)
+    side_blocks = side_blocks.reshape(pair_count, 2, pno_count, fit_rows)
+    orb_total = occ_energy.shape[0]
+    global_orb = region * orb_count + pair_orbs
+    selector = global_orb[:, :, None] == jnp.arange(orb_total, dtype=jnp.int32)[None, None, :]
+    offsets = jnp.sum(jnp.where(selector, fit_offset[None, None, :], 0), axis=2)
+    occupied = jnp.sum(jnp.where(selector, occ_energy[None, None, :], 0.0), axis=2)
+    margin = fit_rows // 4
+    shift_rows = offsets[:, 0] - offsets[:, 1]
+    padded = jnp.pad(side_blocks[:, 1], ((0, 0), (0, 0), (margin, margin)))
+    aligned = jax.vmap(align_rows)(padded, margin + shift_rows)
+    coupling = jnp.einsum(
+        "npr,nqr->npq", side_blocks[:, 0], aligned, preferred_element_type=jnp.float32
+    )
+    denominator = (
+        pno_energy[:, 0, :, None]
+        + pno_energy[:, 1, None, :]
+        - occupied[:, 0, None, None]
+        - occupied[:, 1, None, None]
+    )
+    amplitude = -coupling / denominator
+    energy = jnp.sum(coupling * (2.0 * amplitude - jnp.swapaxes(amplitude, 1, 2)), axis=(1, 2))
+    return (amplitude.reshape(pair_count, pno_count * pno_count), energy)
 
 
 def on_device(raw_ints, fit_inverse, pair_orbs, pno_coef, pno_energy, occ_energy, fit_offset):
@@ -322,50 +494,72 @@
     fit = fit_inverse.shape[1]
     bf16 = jnp.bfloat16
     f32 = jnp.float32
+    i32 = jnp.int32
     vmem = pltpu.VMEM
     dma = pltpu.SemaphoreType.DMA
     smem_spec = pl.BlockSpec(memory_space=pltpu.SMEM)
     vmem_spec = pl.BlockSpec(memory_space=pltpu.VMEM)
     any_spec = pl.BlockSpec(memory_space=pl.ANY)
-    amplitude, energy = pl.pallas_call(
+    amplitude, energy, crowded = pl.pallas_call(
         exchange_kernel,
         out_shape=(
             jax.ShapeDtypeStruct((pairs, npno * npno), f32),
             jax.ShapeDtypeStruct((1, 128), f32),
+            jax.ShapeDtypeStruct((8, 128), i32),
         ),
         in_specs=[smem_spec] * 3 + [vmem_spec] + [any_spec] * 3,
-        out_specs=(vmem_spec, vmem_spec),
+        out_specs=(vmem_spec, vmem_spec, vmem_spec),
         scratch_shapes=[
             vmem((2 * pairs, npno, dom), bf16),
             vmem((fit, fit), bf16),
             vmem((fit, fit), bf16),
             vmem((fit, dom), bf16),
             vmem((dom, fit), bf16),
+            vmem((3, ROW, npno, dom), bf16),
+            vmem((ROW, npno, dom), bf16),
+            vmem((ROW, npno, dom), bf16),
+            vmem((ROW, npno, dom), bf16),
             vmem((4, 4, CAP, npno, dom), bf16),
-            vmem((3, 4, CAP, npno, dom), bf16),
             vmem((4, 3, CAP, npno, dom), bf16),
-            vmem((4, 4, CAP, npno, fit), bf16),
-            vmem((3, 3, CAP, npno, fit), bf16),
-            vmem((4, 4, CAP, npno, fit), bf16),
+            vmem((4, 3, CAP, npno, fit), bf16),
+            vmem((4 * CAP, npno, fit), bf16),
+            vmem((4 * CAP, npno, fit), bf16),
+            vmem((4 * CAP, npno, fit), bf16),
+            vmem((3, ROW, npno, fit), bf16),
+            vmem((4 * CAP + 3 * ROW, npno, fit), bf16),
             vmem((256, fit), bf16),
             vmem((256, fit), bf16),
             vmem((2, npno, pairs * npno), f32),
             vmem((npno, 128), f32),
-            vmem((8, 128), jnp.int32),
-            pltpu.SMEM((8, 128), jnp.int32),
+            vmem((8, 128), i32),
+            vmem((8, 128), i32),
+            vmem((3, 8, 128), i32),
+            vmem((2, 8, 128), i32),
+            vmem((3, 8, 128), i32),
+            vmem((7, 8, 128), i32),
+            pltpu.SMEM((8, 128), i32),
+            pltpu.SMEM((3, 8, 128), i32),
             dma((4,)), dma((7,)), dma((7,)),
-            dma((12,)), dma((12,)), dma((12,)), dma((12,)),
-            dma((12,)), dma((12,)), dma((12,)), dma((12,)),
+            dma((3,)), dma((3,)), dma((12,)), dma((12,)),
+            dma((12,)), dma((12,)), dma((3,)), dma((3,)),
+            dma((3,)), dma((3,)), dma((3,)),
+            dma((3,)), dma((3,)), dma((7,)), dma((7,)),
         ],
         compiler_params=pltpu.CompilerParams(
-            collective_id=0, has_side_effects=True, vmem_limit_bytes=56 * 2**20
+            collective_id=0, has_side_effects=True, vmem_limit_bytes=58 * 2**20
         ),
         name="exchange",
     )(
-        pair_orbs, fit_offset, occ_energy, pno_energy,
+        pair_orbs.T, fit_offset, occ_energy, pno_energy,
         raw_ints, fit_inverse, pno_coef.reshape(2 * pairs, npno, dom),
     )
-    return amplitude, energy[0, :pairs]
+    return lax.cond(
+        crowded[2, 0] > 0,
+        lambda: spread_out(
+            raw_ints, fit_inverse, pair_orbs, pno_coef, pno_energy, occ_energy, fit_offset
+        ),
+        lambda: (amplitude, energy[0, :pairs]),
+    )
 
 
 def solution(mesh):

time: 147 us -> 130 us (0.88)
  the two profiles are of different devices: /device:TPU:18 before, /device:TPU:9 now
where the time goes in v3:
time: 130 us
  Pallas kernels  126 us (97%)
  local copies, waits for them, and re-layouts  1.85 us (1%)
  between operations  1.39 us (1%)
    pallas_call x1, Pallas kernels, on_device(): pl.pallas_call(exchange_kernel, out_shape=(jax.ShapeDtypeStruct((pairs, n...  126 us

profile of v3, /device:TPU:9, one launch (start us, length us, event | category | flops | bytes accessed | tf_op | source)
XLA Modules:
  0.0 129.8 jit_solution(12898631757666104742)
XLA Ops:
  0.6 0.0 copy-start
  0.6 0.0 copy-start.2
  0.7 0.0 copy-start.3
  0.7 0.0 copy-start.4
  0.7 0.0 copy-start.5
  0.7 126.3 %exchange.1 = (f32[16,1024]{1,0:T(8,128)S(1)}, f32[1,128]{1,0:T(1,128)S(1)}, s32[8,128]{1,0:T(8,128)}) custom-call(s32[2,16]{1,0:T(2,128)} %bitcast.68, s32[128]{0:T(128)} %offsets.1, f32[128]{0:T(128)} %occupied.1, f32[16,2,32]{2,1,0:T(2,128)} %levels.1, bf16[8,1,128,1536]{3,2,1,0:T(8,128)(2,1)} %raw_ref.1, bf16[1,1024,1024]{2,1,0:T(8,128)(2,1)} %inv_ref.1, ...), custom_call_target="tpu_custom_call" | custom-call | tf_op jit(solution)/shard_map/exchange/pallas_call | solution.py:503
  127.0 1.2 slice.30
  128.8 0.0 copy-done
  128.8 0.0 copy-done.2
  128.9 0.0 copy-done.3
  128.9 0.0 copy-done.4
  128.9 0.0 copy-done.5
  128.9 0.2 conditional.1
  129.1 0.0 copy-start.7
  129.2 0.6 copy.48
  129.8 0.0 copy-done.7
  (1 shorter events, 0.0 us)
Async XLA Ops:
  0.6 128.2 %copy-start = (bf16[16,2,32,1536]{3,2,1,0:T(8,128)(2,1)S(1)}, bf16[16,2,32,1536]{3,2,1,0:T(8,128)(2,1)}, u32[]{:S(2)}) copy-start(bf16[16,2,32,1536]{3,2,1,0:T(8,128)(2,1)} %param.12) | copy-start | bytes 9437188
  0.6 128.2 %copy-start.2 = (f32[16,2,32]{2,1,0:T(2,128)S(1)}, f32[16,2,32]{2,1,0:T(2,128)}, u32[]{:S(2)}) copy-start(f32[16,2,32]{2,1,0:T(2,128)} %levels.1) | copy-start | bytes 12292
  0.7 128.2 %copy-start.3 = (s32[16,2]{0,1:T(2,128)S(1)}, s32[16,2]{0,1:T(2,128)}, u32[]{:S(2)}) copy-start(s32[16,2]{0,1:T(2,128)} %param.11) | copy-start | bytes 388
  0.7 128.2 %copy-start.4 = (s32[128]{0:T(128)S(1)}, s32[128]{0:T(128)}, u32[]{:S(2)}) copy-start(s32[128]{0:T(128)} %offsets.1) | copy-start | bytes 1540
  0.7 128.2 %copy-start.5 = (f32[128]{0:T(128)S(1)}, f32[128]{0:T(128)}, u32[]{:S(2)}) copy-start(f32[128]{0:T(128)} %occupied.1) | copy-start | bytes 1540
  129.1 0.6 copy-start.7

commit v4 on v3

--- a/solution.py
+++ b/solution.py
@@ -9,8 +9,7 @@
 HOPS = (1, 3, 2)
 RAW_HOPS = ((0, 1), (1, 0), (3, 0), (1, 1), (3, 1), (2, 0), (2, 1))
 CAP = 4
-ROW = 12
-SENDS = {8: 1, 11: 3}
+ROW = 11
 EXACT = lax.Precision.HIGHEST
 
 
@@ -198,7 +197,7 @@
         tell(da)
     load_coef.wait()
     load_table.wait()
-    for da in HOPS:
+    for da in (2, 1, 3):
         to_row = jnp.bitwise_and(own_along + da, 3) * 16
         for q in range(ROW):
             packed_out[da - 1, q] = coef[lookup[2, to_row + q]]
@@ -280,7 +279,7 @@
     for copy in unread:
         copy.wait()
 
-    for da in HOPS:
+    for da in (2, 1, 3):
         first[da].wait_recv()
         for db in (1, 3, 2, 0):
             base = turned(0, db) * CAP
@@ -335,14 +334,23 @@
     for da in HOPS:
         project(away.at[da, 0], back[da].at[pl.ds(0, CAP)])
     project(away.at[0, 0], home.at[pl.ds(0, CAP)])
-    order = [(da, db) for da in (0, 1, 3, 2) for db in HOPS]
-    for i, (da, db) in enumerate(order):
-        second[da, db].wait_recv()
-        project(last.at[da, db - 1], sides.at[da, db - 1])
-        send_third(da, db)
-        if i in SENDS:
-            send_fourth(SENDS[i])
-    send_fourth(2)
+    for db in HOPS:
+        second[0, db].wait_recv()
+        project(last.at[0, db - 1], sides.at[0, db - 1])
+    relays = (2, 1, 3)
+    for i, da in enumerate(relays):
+        for k, db in enumerate(HOPS):
+            second[da, db].wait_recv()
+            project(last.at[da, db - 1], sides.at[da, db - 1])
+            send_third(da, db)
+            if i > 0 and k == 2:
+                send_fourth(relays[i - 1])
+    for db in HOPS:
+        send_third(0, db)
+    if 2 > 2:
+        send_fourth(relays[0])
+        send_fourth(relays[1])
+    send_fourth(relays[2])
     for db in HOPS:
         third[0, db].wait_recv()
     for da in HOPS:
@@ -410,7 +418,7 @@
     for i, copy in enumerate(last_flags):
         copy.wait()
         every_flag = jnp.maximum(every_flag, flags_aux[i])
-    crowded_ref[...] = every_flag
+    crowded_ref[0] = jnp.max(every_flag[2:3])
 
     for copy in raw_copies:
         copy.wait_send()
@@ -505,10 +513,10 @@
         out_shape=(
             jax.ShapeDtypeStruct((pairs, npno * npno), f32),
             jax.ShapeDtypeStruct((1, 128), f32),
-            jax.ShapeDtypeStruct((8, 128), i32),
+            jax.ShapeDtypeStruct((1,), i32),
         ),
         in_specs=[smem_spec] * 3 + [vmem_spec] + [any_spec] * 3,
-        out_specs=(vmem_spec, vmem_spec, vmem_spec),
+        out_specs=(vmem_spec, vmem_spec, smem_spec),
         scratch_shapes=[
             vmem((2 * pairs, npno, dom), bf16),
             vmem((fit, fit), bf16),
@@ -554,7 +562,7 @@
         raw_ints, fit_inverse, pno_coef.reshape(2 * pairs, npno, dom),
     )
     return lax.cond(
-        crowded[2, 0] > 0,
+        crowded[0] > 0,
         lambda: spread_out(
             raw_ints, fit_inverse, pair_orbs, pno_coef, pno_energy, occ_energy, fit_offset
         ),

time: 130 us -> 115 us (0.88)
  the two profiles are of different devices: /device:TPU:9 before, /device:TPU:1 now
where the time goes in v4:
time: 115 us
  Pallas kernels  113 us (98%)
  between operations  1.36 us (1%)
    pallas_call x1, Pallas kernels, on_device(): pl.pallas_call(exchange_kernel, out_shape=(jax.ShapeDtypeStruct((pairs, n...  113 us

profile of v4, /device:TPU:1, one launch (start us, length us, event | category | flops | bytes accessed | tf_op | source)
XLA Modules:
  0.0 115.0 jit_solution(12021572340855103697)
XLA Ops:
  0.6 0.0 copy-start
  0.6 0.0 copy-start.2
  0.7 0.0 copy-start.3
  0.7 0.0 copy-start.4
  0.7 0.0 copy-start.5
  0.7 112.8 %exchange.1 = (f32[16,1024]{1,0:T(8,128)S(1)}, f32[1,128]{1,0:T(1,128)S(1)}, s32[1]{0:T(128)}) custom-call(s32[2,16]{1,0:T(2,128)} %bitcast.68, s32[128]{0:T(128)} %offsets.1, f32[128]{0:T(128)} %occupied.1, f32[16,2,32]{2,1,0:T(2,128)} %levels.1, bf16[8,1,128,1536]{3,2,1,0:T(8,128)(2,1)} %raw_ref.1, bf16[1,1024,1024]{2,1,0:T(8,128)(2,1)} %inv_ref.1, ...), custom_call_target="tpu_custom_call" | custom-call | tf_op jit(solution)/shard_map/exchange/pallas_call | solution.py:511
  114.1 0.0 copy-done
  114.1 0.0 copy-done.2
  114.1 0.0 copy-done.3
  114.1 0.0 copy-done.4
  114.1 0.0 copy-done.5
  114.2 0.2 conditional.1
  114.4 0.0 copy-start.7
  114.4 0.6 copy.48
  115.0 0.0 copy-done.7
  (1 shorter events, 0.0 us)
Async XLA Ops:
  0.6 113.5 %copy-start = (bf16[16,2,32,1536]{3,2,1,0:T(8,128)(2,1)S(1)}, bf16[16,2,32,1536]{3,2,1,0:T(8,128)(2,1)}, u32[]{:S(2)}) copy-start(bf16[16,2,32,1536]{3,2,1,0:T(8,128)(2,1)} %param.12) | copy-start | bytes 9437188
  0.6 113.5 %copy-start.2 = (f32[16,2,32]{2,1,0:T(2,128)S(1)}, f32[16,2,32]{2,1,0:T(2,128)}, u32[]{:S(2)}) copy-start(f32[16,2,32]{2,1,0:T(2,128)} %levels.1) | copy-start | bytes 12292
  0.7 113.5 %copy-start.3 = (s32[16,2]{0,1:T(2,128)S(1)}, s32[16,2]{0,1:T(2,128)}, u32[]{:S(2)}) copy-start(s32[16,2]{0,1:T(2,128)} %param.11) | copy-start | bytes 388
  0.7 113.5 %copy-start.4 = (s32[128]{0:T(128)S(1)}, s32[128]{0:T(128)}, u32[]{:S(2)}) copy-start(s32[128]{0:T(128)} %offsets.1) | copy-start | bytes 1540
  0.7 113.5 %copy-start.5 = (f32[128]{0:T(128)S(1)}, f32[128]{0:T(128)}, u32[]{:S(2)}) copy-start(f32[128]{0:T(128)} %occupied.1) | copy-start | bytes 1540
  114.4 0.6 copy-start.7

commit v5 on v4

--- a/solution.py
+++ b/solution.py
@@ -10,18 +10,19 @@
 RAW_HOPS = ((0, 1), (1, 0), (3, 0), (1, 1), (3, 1), (2, 0), (2, 1))
 CAP = 4
 ROW = 11
+BLOCK = 512
 EXACT = lax.Precision.HIGHEST
 
 
 def exchange_kernel(
     pair_orbs, offsets, occupied, levels, raw_ref, inv_ref, coef_ref,
     out_ref, energy_ref, crowded_ref,
-    coef, inverse, rolled, gathered, fitted_t, packed_out, mid_1, mid_2, mid_3, away, last,
-    sides, back_1, back_2, back_3, packed_back, home,
-    left, right, gap, spread, table, note, notes, flags_out, flags_across, flags_aux,
+    coef, inverse, rolled, gathered, fitted, packed_out, mid_1, mid_2, mid_3, away,
+    back_1, back_2, back_3, packed_back, home,
+    left, right, inside, gap, spread, table, note, notes, flags_out, flags_across, flags_aux,
     lookup, notices,
-    local_sem, raw_send, raw_recv, p1_send, p1_recv, p2_send, p2_recv,
-    r1_send, r1_recv, r2_send, r2_recv, note_send, note_recv, note_sem,
+    local_sem, raw_send, raw_recv, p1_send, p1_recv, fit_send, fit_recv,
+    pass_send, pass_recv, r2_send, r2_recv, note_send, note_recv, note_sem,
     across_send, across_recv, aux_send, aux_recv,
 ):
     mid = {1: mid_1, 2: mid_2, 3: mid_3}
@@ -31,7 +32,8 @@
     x, core = aux // 2, lax.rem(aux, 2)
     y, z = orb // 4, lax.rem(orb, 4)
     fit = inverse.shape[0]
-    dom = fitted_t.shape[0]
+    dom = fitted.shape[1]
+    blocks = dom // BLOCK
     side_count, npno, _ = coef.shape
     pairs = side_count // 2
     rows = raw_ref.shape[2]
@@ -126,22 +128,24 @@
     load_table.start()
 
     pl.semaphore_wait(barrier, 2 * len(HOPS) + len(RAW_HOPS))
-    raw_copies = []
-    for i, hop in enumerate(RAW_HOPS):
-        peer = raw_peer(*hop)
-        raw_copies.append(
-            pltpu.make_async_remote_copy(
-                src_ref=raw_ref.at[peer, 0],
-                dst_ref=gathered.at[pl.ds(aux * rows, rows)],
-                send_sem=raw_send.at[i],
-                recv_sem=raw_recv.at[i],
+    raw_copies = {}
+
+    def send_raw(b):
+        columns = pl.ds(b * BLOCK, BLOCK)
+        for i, hop in enumerate(RAW_HOPS):
+            peer = raw_peer(*hop)
+            raw_copies[b, i] = pltpu.make_async_remote_copy(
+                src_ref=raw_ref.at[peer, 0, :, columns],
+                dst_ref=gathered.at[pl.ds(aux * rows, rows), columns],
+                send_sem=raw_send.at[b * len(RAW_HOPS) + i],
+                recv_sem=raw_recv.at[b * len(RAW_HOPS) + i],
                 device_id=(peer, orb),
                 device_id_type=MESH,
             )
-        )
-        raw_copies[-1].start()
-
-    told, first, second, third, fourth = {}, {}, {}, {}, {}
+            raw_copies[b, i].start()
+
+    send_raw(0)
+    told, first, fourth, shown, passed = {}, {}, {}, {}, {}
 
     def tell(da):
         told[da] = pltpu.make_async_remote_copy(
@@ -159,29 +163,28 @@
         )
         first[da].start()
 
-    def send_second(da, db):
-        k = da * 3 + db - 1
-        second[da, db] = pltpu.make_async_remote_copy(
-            src_ref=away.at[da, db], dst_ref=last.at[da, db - 1],
-            send_sem=p2_send.at[k], recv_sem=p2_recv.at[k],
-            device_id=(aux, turned(0, db)), device_id_type=MESH,
-        )
-        second[da, db].start()
-
-    def send_third(da, db):
-        k = da * 3 + db - 1
-        spots = pl.ds(db * CAP, CAP)
-        third[da, db] = pltpu.make_async_remote_copy(
-            src_ref=sides.at[da, db - 1],
-            dst_ref=home.at[spots] if da == 0 else back[da].at[spots],
-            send_sem=r1_send.at[k], recv_sem=r1_recv.at[k],
-            device_id=(aux, turned(0, 4 - db)), device_id_type=MESH,
-        )
-        third[da, db].start()
+    def show(b):
+        span = pl.ds(b * BLOCK, BLOCK)
+        for k, db in enumerate((1, 3)):
+            shown[b, db] = pltpu.make_async_remote_copy(
+                src_ref=fitted.at[0, span], dst_ref=fitted.at[4 - db, span],
+                send_sem=fit_send.at[2 * b + k], recv_sem=fit_recv.at[2 * b + k],
+                device_id=(aux, turned(0, db)), device_id_type=MESH,
+            )
+            shown[b, db].start()
+
+    def pass_on(b):
+        for k, db in enumerate((1, 3)):
+            shown[b, db].wait_recv()
+            span = pl.ds(b * BLOCK + k * (BLOCK // 2), BLOCK // 2)
+            passed[b, db] = pltpu.make_async_remote_copy(
+                src_ref=fitted.at[4 - db, span], dst_ref=fitted.at[2, span],
+                send_sem=pass_send.at[2 * b + k], recv_sem=pass_recv.at[2 * b + k],
+                device_id=(aux, turned(0, db)), device_id_type=MESH,
+            )
+            passed[b, db].start()
 
     def send_fourth(da):
-        for db in HOPS:
-            third[da, db].wait_recv()
         at = (own_along * 16)
         for q in range(ROW):
             packed_back[da - 1, q] = back[da][notices[da - 1, 1, at + q]]
@@ -202,12 +205,12 @@
         for q in range(ROW):
             packed_out[da - 1, q] = coef[lookup[2, to_row + q]]
         send_first(da)
-    for db in (1, 3, 2, 0):
+    for db in range(4):
         base = turned(0, db) * CAP
         for j in range(CAP):
             away[0, db, j] = coef[lookup[0, base + j]]
-        if db != 0:
-            send_second(0, db)
+    if blocks > 1:
+        send_raw(1)
 
     wide = pairs * npno
     of_lane = lax.broadcasted_iota(jnp.int32, (pairs, wide), 1) // npno
@@ -238,6 +241,14 @@
         along_lanes.append(jnp.sum(jnp.where(in_pair, every, 0.0), axis=0, keepdims=True))
     gap[0] = down[0] + along_lanes[1] - filled
     gap[1] = down[1] + along_lanes[0] - filled
+
+    fit_lane = lax.broadcasted_iota(jnp.int32, (16, fit), 1)
+    for n in range(pairs):
+        off_0 = offsets[aux * 16 + pair_orbs[0, n]]
+        off_1 = offsets[aux * 16 + pair_orbs[1, n]]
+        low, high = jnp.minimum(off_0, off_1), jnp.maximum(off_0, off_1)
+        outside = jnp.logical_and(fit_lane >= low, fit_lane < high)
+        inside[n] = jnp.where(outside, 0.0, 1.0).astype(jnp.bfloat16)
 
     load_inverse.wait()
     own_offset = offsets[aux * 16 + orb]
@@ -279,15 +290,6 @@
     for copy in unread:
         copy.wait()
 
-    for da in (2, 1, 3):
-        first[da].wait_recv()
-        for db in (1, 3, 2, 0):
-            base = turned(0, db) * CAP
-            for j in range(CAP):
-                away[da, db, j] = mid[da][notices[da - 1, 0, base + j]]
-            if db != 0:
-                send_second(da, db)
-
     for copy in flag_copies:
         copy.wait()
     flags_out[1] = jnp.maximum(
@@ -306,60 +308,70 @@
         last_flags[-1].start()
 
     load_own.wait()
-    for copy in raw_copies:
-        copy.wait_recv()
-
-    def fit_tile(n, carry):
-        start = pl.multiple_of(n * tile, tile)
-        block = jnp.dot(
-            rolled[...], gathered[:, pl.ds(start, tile)], preferred_element_type=jnp.float32
-        ).astype(jnp.bfloat16)
-        fitted_t[pl.ds(start, tile), :] = block.T
-        return carry
-
-    lax.fori_loop(0, dom // tile, fit_tile, 0)
-
-    def project(source, target):
+    for b in range(blocks):
+        for i in range(len(RAW_HOPS)):
+            raw_copies[b, i].wait_recv()
+        if b + 2 < blocks:
+            send_raw(b + 2)
+
+        def fit_tile(n, carry):
+            start = pl.multiple_of(b * BLOCK + n * tile, tile)
+            block = jnp.dot(
+                rolled[...], gathered[:, pl.ds(start, tile)],
+                preferred_element_type=jnp.float32,
+            ).astype(jnp.bfloat16)
+            fitted[0, pl.ds(start, tile), :] = block.T
+            return carry
+
+        lax.fori_loop(0, BLOCK // tile, fit_tile, 0)
+        show(b)
+        if b > 0:
+            pass_on(b - 1)
+
+    for da in (2, 1, 3):
+        first[da].wait_recv()
+        for db in range(4):
+            base = turned(0, db) * CAP
+            for j in range(CAP):
+                away[da, db, j] = mid[da][notices[da - 1, 0, base + j]]
+
+    def project(source, db, target):
         def columns(n, carry):
             start = pl.multiple_of(n * tile, tile)
             lhs = source[...].reshape(CAP * npno, dom)
             block = jnp.dot(
-                lhs, fitted_t[:, pl.ds(start, tile)], preferred_element_type=jnp.float32
+                lhs, fitted[db, :, pl.ds(start, tile)], preferred_element_type=jnp.float32
             ).astype(jnp.bfloat16)
             target[:, :, pl.ds(start, tile)] = block.reshape(CAP, npno, tile)
             return carry
 
         lax.fori_loop(0, fit // tile, columns, 0)
 
-    for da in HOPS:
-        project(away.at[da, 0], back[da].at[pl.ds(0, CAP)])
-    project(away.at[0, 0], home.at[pl.ds(0, CAP)])
-    for db in HOPS:
-        second[0, db].wait_recv()
-        project(last.at[0, db - 1], sides.at[0, db - 1])
-    relays = (2, 1, 3)
-    for i, da in enumerate(relays):
-        for k, db in enumerate(HOPS):
-            second[da, db].wait_recv()
-            project(last.at[da, db - 1], sides.at[da, db - 1])
-            send_third(da, db)
-            if i > 0 and k == 2:
-                send_fourth(relays[i - 1])
-    for db in HOPS:
-        send_third(0, db)
-    if 2 > 2:
-        send_fourth(relays[0])
-        send_fourth(relays[1])
-    send_fourth(relays[2])
-    for db in HOPS:
-        third[0, db].wait_recv()
+    def project_all(da, db):
+        spots = pl.ds(db * CAP, CAP)
+        project(away.at[da, db], db, home.at[spots] if da == 0 else back[da].at[spots])
+
+    everyone = (2, 1, 3, 0)
+    for da in everyone[:2]:
+        project_all(da, 0)
+    pass_on(blocks - 1)
+    for da in everyone[2:]:
+        project_all(da, 0)
+    for db in (1, 3):
+        for da in everyone:
+            project_all(da, db)
+    for copy in passed.values():
+        copy.wait_recv()
+    for da in everyone:
+        project_all(da, 2)
+        if da != 0:
+            send_fourth(da)
     for da in HOPS:
         fourth[da].wait_recv()
 
     per = tile // npno
     lanes = 128
     packed = lanes // npno
-    fit_lane = lax.broadcasted_iota(jnp.int32, (npno, fit), 1)
     block_of = lax.broadcasted_iota(jnp.int32, (npno, lanes), 1) // npno
     contract = (((1,), (1,)), ((), ()))
     energies = jnp.zeros((1, lanes), jnp.float32)
@@ -367,19 +379,16 @@
     for half in range(pairs // per):
         for i in range(per):
             n = half * per + i
-            off_0 = offsets[aux * 16 + pair_orbs[0, n]]
-            off_1 = offsets[aux * 16 + pair_orbs[1, n]]
-            low, high = jnp.minimum(off_0, off_1), jnp.maximum(off_0, off_1)
             one = home[lookup[1, 2 * n]]
-            outside = jnp.logical_and(fit_lane >= low, fit_lane < high)
-            left[pl.ds(i * npno, npno), :] = jnp.where(outside, jnp.zeros_like(one), one)
+            for part in range(npno // 16):
+                left[pl.ds(i * npno + part * 16, 16), :] = (
+                    one[part * 16:(part + 1) * 16] * inside[n]
+                )
             right[pl.ds(i * npno, npno), :] = home[lookup[1, 2 * n + 1]]
         ahead = lax.dot_general(
             left[...], right[...], contract, preferred_element_type=jnp.float32
         )
-        behind = lax.dot_general(
-            right[...], left[...], contract, preferred_element_type=jnp.float32
-        )
+        behind = ahead.T
         for part in range(per // packed):
             forward = jnp.zeros((npno, lanes), jnp.float32)
             swapped = jnp.zeros((npno, lanes), jnp.float32)
@@ -420,9 +429,7 @@
         every_flag = jnp.maximum(every_flag, flags_aux[i])
     crowded_ref[0] = jnp.max(every_flag[2:3])
 
-    for copy in raw_copies:
-        copy.wait_send()
-    for group in (told, first, second, third, fourth):
+    for group in (raw_copies, told, first, shown, passed, fourth):
         for copy in group.values():
             copy.wait_send()
 
@@ -503,6 +510,7 @@
     bf16 = jnp.bfloat16
     f32 = jnp.float32
     i32 = jnp.int32
+    blocks = dom // BLOCK
     vmem = pltpu.VMEM
     dma = pltpu.SemaphoreType.DMA
     smem_spec = pl.BlockSpec(memory_space=pltpu.SMEM)
@@ -522,14 +530,12 @@
             vmem((fit, fit), bf16),
             vmem((fit, fit), bf16),
             vmem((fit, dom), bf16),
-            vmem((dom, fit), bf16),
+            vmem((4, dom, fit), bf16),
             vmem((3, ROW, npno, dom), bf16),
             vmem((ROW, npno, dom), bf16),
             vmem((ROW, npno, dom), bf16),
             vmem((ROW, npno, dom), bf16),
             vmem((4, 4, CAP, npno, dom), bf16),
-            vmem((4, 3, CAP, npno, dom), bf16),
-            vmem((4, 3, CAP, npno, fit), bf16),
             vmem((4 * CAP, npno, fit), bf16),
             vmem((4 * CAP, npno, fit), bf16),
             vmem((4 * CAP, npno, fit), bf16),
@@ -537,6 +543,7 @@
             vmem((4 * CAP + 3 * ROW, npno, fit), bf16),
             vmem((256, fit), bf16),
             vmem((256, fit), bf16),
+            vmem((pairs, 16, fit), bf16),
             vmem((2, npno, pairs * npno), f32),
             vmem((npno, 128), f32),
             vmem((8, 128), i32),
@@ -547,9 +554,9 @@
             vmem((7, 8, 128), i32),
             pltpu.SMEM((8, 128), i32),
             pltpu.SMEM((3, 8, 128), i32),
-            dma((4,)), dma((7,)), dma((7,)),
-            dma((3,)), dma((3,)), dma((12,)), dma((12,)),
-            dma((12,)), dma((12,)), dma((3,)), dma((3,)),
+            dma((4,)), dma((7 * blocks,)), dma((7 * blocks,)),
+            dma((3,)), dma((3,)), dma((2 * blocks,)), dma((2 * blocks,)),
+            dma((2 * blocks,)), dma((2 * blocks,)), dma((3,)), dma((3,)),
             dma((3,)), dma((3,)), dma((3,)),
             dma((3,)), dma((3,)), dma((7,)), dma((7,)),
         ],

time: 115 us -> 111 us (0.965)
  Pallas kernels: 113 us -> 108 us
    pallas_call x1, Pallas kernels: 113 us -> 108 us  [on_device(): pl.pallas_call(exchange_kernel, out_shape=(jax.ShapeDtypeStruct((pairs, n...]
where the time goes in v5:
time: 111 us
  Pallas kernels  108 us (97%)
  between operations  1.36 us (1%)
    pallas_call x1, Pallas kernels, on_device(): pl.pallas_call(exchange_kernel, out_shape=(jax.ShapeDtypeStruct((pairs, n...  108 us

profile of v5, /device:TPU:1, one launch (start us, length us, event | category | flops | bytes accessed | tf_op | source)
XLA Modules:
  0.0 110.5 jit_solution(17835893621141636606)
XLA Ops:
  0.6 0.0 copy-start
  0.6 0.0 copy-start.2
  0.7 0.0 copy-start.3
  0.7 0.0 copy-start.4
  0.7 0.0 copy-start.5
  0.7 108.2 %exchange.1 = (f32[16,1024]{1,0:T(8,128)S(1)}, f32[1,128]{1,0:T(1,128)S(1)}, s32[1]{0:T(128)}) custom-call(s32[2,16]{1,0:T(2,128)} %bitcast.68, s32[128]{0:T(128)} %offsets.1, f32[128]{0:T(128)} %occupied.1, f32[16,2,32]{2,1,0:T(2,128)} %levels.1, bf16[8,1,128,1536]{3,2,1,0:T(8,128)(2,1)} %raw_ref.1, bf16[1,1024,1024]{2,1,0:T(8,128)(2,1)} %inv_ref.1, ...), custom_call_target="tpu_custom_call" | custom-call | tf_op jit(solution)/shard_map/exchange/pallas_call | solution.py:519
  109.6 0.0 copy-done
  109.6 0.0 copy-done.2
  109.6 0.0 copy-done.3
  109.6 0.0 copy-done.4
  109.6 0.0 copy-done.5
  109.6 0.2 conditional.1
  109.9 0.0 copy-start.7
  109.9 0.6 copy.48
  110.5 0.0 copy-done.7
  (1 shorter events, 0.0 us)
Async XLA Ops:
  0.6 108.9 %copy-start = (bf16[16,2,32,1536]{3,2,1,0:T(8,128)(2,1)S(1)}, bf16[16,2,32,1536]{3,2,1,0:T(8,128)(2,1)}, u32[]{:S(2)}) copy-start(bf16[16,2,32,1536]{3,2,1,0:T(8,128)(2,1)} %param.12) | copy-start | bytes 9437188
  0.6 108.9 %copy-start.2 = (f32[16,2,32]{2,1,0:T(2,128)S(1)}, f32[16,2,32]{2,1,0:T(2,128)}, u32[]{:S(2)}) copy-start(f32[16,2,32]{2,1,0:T(2,128)} %levels.1) | copy-start | bytes 12292
  0.7 108.9 %copy-start.3 = (s32[16,2]{0,1:T(2,128)S(1)}, s32[16,2]{0,1:T(2,128)}, u32[]{:S(2)}) copy-start(s32[16,2]{0,1:T(2,128)} %param.11) | copy-start | bytes 388
  0.7 108.9 %copy-start.4 = (s32[128]{0:T(128)S(1)}, s32[128]{0:T(128)}, u32[]{:S(2)}) copy-start(s32[128]{0:T(128)} %offsets.1) | copy-start | bytes 1540
  0.7 108.9 %copy-start.5 = (f32[128]{0:T(128)S(1)}, f32[128]{0:T(128)}, u32[]{:S(2)}) copy-start(f32[128]{0:T(128)} %occupied.1) | copy-start | bytes 1540
  109.9 0.6 copy-start.7

commit v6 on v5

--- a/solution.py
+++ b/solution.py
@@ -10,6 +10,9 @@
 RAW_HOPS = ((0, 1), (1, 0), (3, 0), (1, 1), (3, 1), (2, 0), (2, 1))
 CAP = 4
 ROW = 11
+NEAR = 14
+FAR = 6
+FAR_AT = 1
 BLOCK = 512
 EXACT = lax.Precision.HIGHEST
 
@@ -17,7 +20,7 @@
 def exchange_kernel(
     pair_orbs, offsets, occupied, levels, raw_ref, inv_ref, coef_ref,
     out_ref, energy_ref, crowded_ref,
-    coef, inverse, rolled, gathered, fitted, packed_out, mid_1, mid_2, mid_3, away,
+    coef, inverse, rolled, gathered, fitted, packed_out, packed_far, mid_1, mid_2, mid_3, away,
     back_1, back_2, back_3, packed_back, home,
     left, right, inside, gap, spread, table, note, notes, flags_out, flags_across, flags_aux,
     lookup, notices,
@@ -116,13 +119,55 @@
         jnp.bitwise_and(place_in_row(list_orb) + 4 - own_across, 3) * CAP
         + jnp.minimum(list_spot, CAP - 1)
     )
-    crowded = jnp.max(jnp.where(jnp.logical_and(list_row < 4, seen_list > ROW), 1, 0))
+    def named(step):
+        there = list_row == jnp.bitwise_and(own_along + step, 3)
+        return jnp.max(jnp.where(there, seen_list, 0))
+
+    ahead_count, far_count, behind_count = named(1), named(2), named(3)
+    by_ahead = jnp.minimum(jnp.minimum(far_count, FAR), jnp.maximum(NEAR - ahead_count, 0))
+    by_behind = far_count - by_ahead
+    fits = jnp.logical_and(
+        jnp.logical_and(ahead_count <= ROW, behind_count <= ROW),
+        jnp.logical_and(
+            far_count <= ROW,
+            jnp.logical_and(by_behind <= FAR, behind_count + by_behind <= NEAR),
+        ),
+    )
+    crowded = jnp.where(fits, 0, 1)
+    in_far = slot_row == jnp.bitwise_and(own_along + 2, 3)
+    slot_list = jnp.where(
+        in_far,
+        jnp.where(slot_list < by_ahead, slot_list, slot_list - by_ahead + FAR),
+        slot_list,
+    )
     row_at = lax.broadcasted_iota(jnp.int32, (8, 128), 0)
-    table[...] = jnp.where(row_at == 0, in_slot, jnp.where(row_at == 1, home_slot, in_list))
+    table[...] = jnp.where(
+        row_at == 0,
+        in_slot,
+        jnp.where(
+            row_at == 1,
+            home_slot,
+            jnp.where(
+                row_at == 2,
+                in_list,
+                jnp.where(
+                    row_at == 3, ahead_count, jnp.where(row_at == 4, behind_count, by_ahead)
+                ),
+            ),
+        ),
+    )
     note[...] = jnp.where(
         row_at == 0,
-        jnp.minimum(slot_list, ROW - 1),
-        jnp.where(row_at == 1, list_slot, crowded),
+        jnp.minimum(slot_list, 2 * FAR - 1),
+        jnp.where(
+            row_at == 1,
+            list_slot,
+            jnp.where(
+                row_at == 2,
+                crowded,
+                jnp.where(row_at == 3, ahead_count, behind_count),
+            ),
+        ),
     )
     load_table = pltpu.make_async_copy(table, lookup, local_sem.at[3])
     load_table.start()
@@ -145,7 +190,7 @@
             raw_copies[b, i].start()
 
     send_raw(0)
-    told, first, fourth, shown, passed = {}, {}, {}, {}, {}
+    told, first, far, fourth, shown, passed = {}, {}, {}, {}, {}, {}
 
     def tell(da):
         told[da] = pltpu.make_async_remote_copy(
@@ -156,12 +201,26 @@
         told[da].start()
 
     def send_first(da):
+        k = da // 2
         first[da] = pltpu.make_async_remote_copy(
-            src_ref=packed_out.at[da - 1], dst_ref=mid[da],
-            send_sem=p1_send.at[da - 1], recv_sem=p1_recv.at[da - 1],
+            src_ref=packed_out.at[k], dst_ref=mid[da],
+            send_sem=p1_send.at[k], recv_sem=p1_recv.at[k],
             device_id=(aux, turned(da, 0)), device_id_type=MESH,
         )
         first[da].start()
+
+    def send_far(da):
+        k = da // 2
+        first[da].wait_recv()
+        start = notices[da - 1, 3 + k, 0]
+        for q in range(FAR):
+            packed_far[k, q] = mid[da][jnp.minimum(start + q, NEAR - 1)]
+        far[da] = pltpu.make_async_remote_copy(
+            src_ref=packed_far.at[k], dst_ref=mid[2].at[pl.ds(k * FAR, FAR)],
+            send_sem=p1_send.at[2 + k], recv_sem=p1_recv.at[2 + k],
+            device_id=(aux, turned(da, 0)), device_id_type=MESH,
+        )
+        far[da].start()
 
     def show(b):
         span = pl.ds(b * BLOCK, BLOCK)
@@ -200,10 +259,15 @@
         tell(da)
     load_coef.wait()
     load_table.wait()
-    for da in (2, 1, 3):
+    far_row = jnp.bitwise_and(own_along + 2, 3) * 16
+    for da in (1, 3):
         to_row = jnp.bitwise_and(own_along + da, 3) * 16
-        for q in range(ROW):
-            packed_out[da - 1, q] = coef[lookup[2, to_row + q]]
+        near_count = lookup[3 + da // 2, 0]
+        skipped = lookup[5, 0] if da == 3 else 0
+        for q in range(NEAR):
+            beyond = jnp.clip(q - near_count + skipped, 0, 15)
+            at = jnp.where(q < near_count, to_row + q, far_row + beyond)
+            packed_out[da // 2, q] = coef[lookup[2, at]]
         send_first(da)
     for db in range(4):
         base = turned(0, db) * CAP
@@ -325,11 +389,16 @@
 
         lax.fori_loop(0, BLOCK // tile, fit_tile, 0)
         show(b)
+        if b == FAR_AT:
+            for da in (1, 3):
+                send_far(da)
         if b > 0:
             pass_on(b - 1)
 
-    for da in (2, 1, 3):
-        first[da].wait_recv()
+    for da in (1, 3, 2):
+        if da == 2:
+            for copy in far.values():
+                copy.wait_recv()
         for db in range(4):
             base = turned(0, db) * CAP
             for j in range(CAP):
@@ -429,7 +498,7 @@
         every_flag = jnp.maximum(every_flag, flags_aux[i])
     crowded_ref[0] = jnp.max(every_flag[2:3])
 
-    for group in (raw_copies, told, first, shown, passed, fourth):
+    for group in (raw_copies, told, first, far, shown, passed, fourth):
         for copy in group.values():
             copy.wait_send()
 
@@ -531,10 +600,11 @@
             vmem((fit, fit), bf16),
             vmem((fit, dom), bf16),
             vmem((4, dom, fit), bf16),
-            vmem((3, ROW, npno, dom), bf16),
-            vmem((ROW, npno, dom), bf16),
-            vmem((ROW, npno, dom), bf16),
-            vmem((ROW, npno, dom), bf16),
+            vmem((2, NEAR, npno, dom), bf16),
+            vmem((2, FAR, npno, dom), bf16),
+            vmem((NEAR, npno, dom), bf16),
+            vmem((2 * FAR, npno, dom), bf16),
+            vmem((NEAR, npno, dom), bf16),
             vmem((4, 4, CAP, npno, dom), bf16),
             vmem((4 * CAP, npno, fit), bf16),
             vmem((4 * CAP, npno, fit), bf16),
@@ -555,7 +625,7 @@
             pltpu.SMEM((8, 128), i32),
             pltpu.SMEM((3, 8, 128), i32),
             dma((4,)), dma((7 * blocks,)), dma((7 * blocks,)),
-            dma((3,)), dma((3,)), dma((2 * blocks,)), dma((2 * blocks,)),
+            dma((4,)), dma((4,)), dma((2 * blocks,)), dma((2 * blocks,)),
             dma((2 * blocks,)), dma((2 * blocks,)), dma((3,)), dma((3,)),
             dma((3,)), dma((3,)), dma((3,)),
             dma((3,)), dma((3,)), dma((7,)), dma((7,)),

time: 111 us -> 109 us (0.982)
  Pallas kernels: 108 us -> 106 us
    pallas_call x1, Pallas kernels: 108 us -> 106 us  [on_device(): pl.pallas_call(exchange_kernel, out_shape=(jax.ShapeDtypeStruct((pairs, n...]
where the time goes in v6:
time: 109 us
  Pallas kernels  106 us (97%)
  between operations  1.36 us (1%)
    pallas_call x1, Pallas kernels, on_device(): pl.pallas_call(exchange_kernel, out_shape=(jax.ShapeDtypeStruct((pairs, n...  106 us

profile of v6, /device:TPU:1, one launch (start us, length us, event | category | flops | bytes accessed | tf_op | source)
XLA Modules:
  0.0 108.6 jit_solution(17897659064406192905)
XLA Ops:
  0.6 0.0 copy-start
  0.6 0.0 copy-start.2
  0.7 0.0 copy-start.3
  0.7 0.0 copy-start.4
  0.7 0.0 copy-start.5
  0.7 106.3 %exchange.1 = (f32[16,1024]{1,0:T(8,128)S(1)}, f32[1,128]{1,0:T(1,128)S(1)}, s32[1]{0:T(128)}) custom-call(s32[2,16]{1,0:T(2,128)} %bitcast.68, s32[128]{0:T(128)} %offsets.1, f32[128]{0:T(128)} %occupied.1, f32[16,2,32]{2,1,0:T(2,128)} %levels.1, bf16[8,1,128,1536]{3,2,1,0:T(8,128)(2,1)} %raw_ref.1, bf16[1,1024,1024]{2,1,0:T(8,128)(2,1)} %inv_ref.1, ...), custom_call_target="tpu_custom_call" | custom-call | tf_op jit(solution)/shard_map/exchange/pallas_call | solution.py:588
  107.6 0.0 copy-done
  107.7 0.0 copy-done.2
  107.7 0.0 copy-done.3
  107.7 0.0 copy-done.4
  107.7 0.0 copy-done.5
  107.7 0.2 conditional.1
  107.9 0.0 copy-start.7
  108.0 0.6 copy.48
  108.6 0.0 copy-done.7
  (1 shorter events, 0.0 us)
Async XLA Ops:
  0.6 107.0 %copy-start = (bf16[16,2,32,1536]{3,2,1,0:T(8,128)(2,1)S(1)}, bf16[16,2,32,1536]{3,2,1,0:T(8,128)(2,1)}, u32[]{:S(2)}) copy-start(bf16[16,2,32,1536]{3,2,1,0:T(8,128)(2,1)} %param.12) | copy-start | bytes 9437188
  0.6 107.0 %copy-start.2 = (f32[16,2,32]{2,1,0:T(2,128)S(1)}, f32[16,2,32]{2,1,0:T(2,128)}, u32[]{:S(2)}) copy-start(f32[16,2,32]{2,1,0:T(2,128)} %levels.1) | copy-start | bytes 12292
  0.7 107.0 %copy-start.3 = (s32[16,2]{0,1:T(2,128)S(1)}, s32[16,2]{0,1:T(2,128)}, u32[]{:S(2)}) copy-start(s32[16,2]{0,1:T(2,128)} %param.11) | copy-start | bytes 388
  0.7 107.0 %copy-start.4 = (s32[128]{0:T(128)S(1)}, s32[128]{0:T(128)}, u32[]{:S(2)}) copy-start(s32[128]{0:T(128)} %offsets.1) | copy-start | bytes 1540
  0.7 107.0 %copy-start.5 = (f32[128]{0:T(128)S(1)}, f32[128]{0:T(128)}, u32[]{:S(2)}) copy-start(f32[128]{0:T(128)} %occupied.1) | copy-start | bytes 1540
  107.9 0.6 copy-start.7

commit v7 on v6

--- a/solution.py
+++ b/solution.py
@@ -272,7 +272,7 @@
     for db in range(4):
         base = turned(0, db) * CAP
         for j in range(CAP):
-            away[0, db, j] = coef[lookup[0, base + j]]
+            away[db, 0, j] = coef[lookup[0, base + j]]
     if blocks > 1:
         send_raw(1)
 
@@ -402,7 +402,7 @@
         for db in range(4):
             base = turned(0, db) * CAP
             for j in range(CAP):
-                away[da, db, j] = mid[da][notices[da - 1, 0, base + j]]
+                away[db, da, j] = mid[da][notices[da - 1, 0, base + j]]
 
     def project(source, db, target):
         def columns(n, carry):
@@ -418,17 +418,30 @@
 
     def project_all(da, db):
         spots = pl.ds(db * CAP, CAP)
-        project(away.at[da, db], db, home.at[spots] if da == 0 else back[da].at[spots])
+        project(away.at[db, da], db, home.at[spots] if da == 0 else back[da].at[spots])
 
     everyone = (2, 1, 3, 0)
-    for da in everyone[:2]:
-        project_all(da, 0)
+
+    def project_group(db):
+        spots = pl.ds(db * CAP, CAP)
+
+        def columns(n, carry):
+            span = pl.ds(pl.multiple_of(n * tile, tile), tile)
+            block = jnp.dot(
+                away[db].reshape(4 * CAP * npno, dom), fitted[db, :, span],
+                preferred_element_type=jnp.float32,
+            ).astype(jnp.bfloat16).reshape(4, CAP, npno, tile)
+            home[spots, :, span] = block[0]
+            for da in HOPS:
+                back[da][spots, :, span] = block[da]
+            return carry
+
+        lax.fori_loop(0, fit // tile, columns, 0)
+
+    project_group(0)
     pass_on(blocks - 1)
-    for da in everyone[2:]:
-        project_all(da, 0)
-    for db in (1, 3):
-        for da in everyone:
-            project_all(da, db)
+    project_group(1)
+    project_group(3)
     for copy in passed.values():
         copy.wait_recv()
     for da in everyone:

time: 109 us -> 108 us (level)
  no operation moved by 1% of the time
where the time goes in v7:
time: 108 us
  Pallas kernels  106 us (98%)
  between operations  1.36 us (1%)
    pallas_call x1, Pallas kernels, on_device(): pl.pallas_call(exchange_kernel, out_shape=(jax.ShapeDtypeStruct((pairs, n...  106 us

profile of v7, /device:TPU:1, one launch (start us, length us, event | category | flops | bytes accessed | tf_op | source)
XLA Modules:
  0.0 108.2 jit_solution(10724633423033087569)
XLA Ops:
  0.6 0.0 copy-start
  0.6 0.0 copy-start.2
  0.7 0.0 copy-start.3
  0.7 0.0 copy-start.4
  0.7 0.0 copy-start.5
  0.7 105.9 %exchange.1 = (f32[16,1024]{1,0:T(8,128)S(1)}, f32[1,128]{1,0:T(1,128)S(1)}, s32[1]{0:T(128)}) custom-call(s32[2,16]{1,0:T(2,128)} %bitcast.68, s32[128]{0:T(128)} %offsets.1, f32[128]{0:T(128)} %occupied.1, f32[16,2,32]{2,1,0:T(2,128)} %levels.1, bf16[8,1,128,1536]{3,2,1,0:T(8,128)(2,1)} %raw_ref.1, bf16[1,1024,1024]{2,1,0:T(8,128)(2,1)} %inv_ref.1, ...), custom_call_target="tpu_custom_call" | custom-call | tf_op jit(solution)/shard_map/exchange/pallas_call | solution.py:601
  107.2 0.0 copy-done
  107.3 0.0 copy-done.2
  107.3 0.0 copy-done.3
  107.3 0.0 copy-done.4
  107.3 0.0 copy-done.5
  107.3 0.2 conditional.1
  107.5 0.0 copy-start.7
  107.6 0.6 copy.48
  108.2 0.0 copy-done.7
  (1 shorter events, 0.0 us)
Async XLA Ops:
  0.6 106.6 %copy-start = (bf16[16,2,32,1536]{3,2,1,0:T(8,128)(2,1)S(1)}, bf16[16,2,32,1536]{3,2,1,0:T(8,128)(2,1)}, u32[]{:S(2)}) copy-start(bf16[16,2,32,1536]{3,2,1,0:T(8,128)(2,1)} %param.12) | copy-start | bytes 9437188
  0.6 106.6 %copy-start.2 = (f32[16,2,32]{2,1,0:T(2,128)S(1)}, f32[16,2,32]{2,1,0:T(2,128)}, u32[]{:S(2)}) copy-start(f32[16,2,32]{2,1,0:T(2,128)} %levels.1) | copy-start | bytes 12292
  0.7 106.6 %copy-start.3 = (s32[16,2]{0,1:T(2,128)S(1)}, s32[16,2]{0,1:T(2,128)}, u32[]{:S(2)}) copy-start(s32[16,2]{0,1:T(2,128)} %param.11) | copy-start | bytes 388
  0.7 106.6 %copy-start.4 = (s32[128]{0:T(128)S(1)}, s32[128]{0:T(128)}, u32[]{:S(2)}) copy-start(s32[128]{0:T(128)} %offsets.1) | copy-start | bytes 1540
  0.7 106.6 %copy-start.5 = (f32[128]{0:T(128)S(1)}, f32[128]{0:T(128)}, u32[]{:S(2)}) copy-start(f32[128]{0:T(128)} %occupied.1) | copy-start | bytes 1540
  107.5 0.6 copy-start.7
